TPU v7x, 32 devices: a whole 2x2x4 slice. The times are simulated.
32 devices in a mesh: atm: 8 (over z, x), cpl: 4 (over y, core).
Axes of the slice: x: 2, y: 2, z: 4, core: 2. Of those that a mesh axis runs over, the one named last changes fastest.
Arguments:
- state: bfloat16 [16384, 32, 128], P(('atm', 'cpl')), may hold values from -6 to 6
- cosine_zenith: bfloat16 [16384], P(('atm', 'cpl')), may hold values from 0.25 to 1
- sunlit: int32 [16384], P(('atm', 'cpl')), may hold values from 0 to 1, as said below
- kcoef: bfloat16 [32, 256], replicated, may hold values from -1 to 1
- scatter_coef: bfloat16 [32, 256], replicated, may hold values from -1 to 1
- gpoint_weight: float32 [256], replicated, may hold values from 0.3 to 3
- sea_temp: float32 [16384], P(('atm', 'cpl')), may hold values from -6 to 6
- intersection_col: int32 [16384, 4], P(('atm', 'cpl')), may hold values from 0 to 2047
- intersection_weight: int32 [16384, 4], P(('atm', 'cpl')), may hold values from 1 to 8
- nearest_ocean: int32 [16384], P(('atm', 'cpl')), may hold values from 0 to 2047
Outputs:
- heating_rate: float32 [16384, 128], P(('atm', 'cpl'))
- sea_temp_next: float32 [16384], P(('atm', 'cpl'))
- column_sea_temp: float32 [16384], P(('atm', 'cpl'))
Inputs may be any that keep to these rules, and one draw needn't show every extreme that they name: On each device the number of sunlit columns is a multiple of 8; the two devices of one cpl index whose atm indices differ by 4 together hold exactly 512 sunlit columns. `intersection_col`: Indexes, in cpl order, the columns held by the 4 devices that share the ocean cell's atm index. `nearest_ocean`: Indexes, in cpl order, the ocean cells held by the 4 devices that share the column's atm index.
All inputs are finite; a program needn't handle non-finite values.
Results may differ from a plain program's by a relative error of at most 0.0006.
Values may be sent and summed in bfloat16 or wider, within the bound.
A program may use at most 64 MiB of HBM per device.

v0:
```python
import jax
import jax.numpy as jnp
from jax import lax
from jax.sharding import PartitionSpec as P

depth_scale = 0.01
relax_keep = 0.75
forcing = 4.0
block_cols = 32


def column_optics(state_blk, cosine_blk, kcoef, scatter_coef, weights):
    levels = state_blk.shape[2]
    gpoints = kcoef.shape[1]
    proj_abs = jnp.einsum("cfl,fg->clg", state_blk, kcoef, preferred_element_type=jnp.float32)
    proj_sca = jnp.einsum(
        "cfl,fg->clg", state_blk, scatter_coef, preferred_element_type=jnp.float32
    )
    soft_abs = jax.nn.softplus(proj_abs)
    soft_sca = jax.nn.softplus(proj_sca)
    extinction = (depth_scale * (soft_abs + soft_sca)).astype(jnp.bfloat16)
    share = soft_abs / (soft_abs + soft_sca)
    row_index = lax.broadcasted_iota(jnp.int32, (levels, levels), 0)
    col_index = lax.broadcasted_iota(jnp.int32, (levels, levels), 1)
    upper = (row_index < col_index).astype(jnp.bfloat16)
    above = jnp.einsum("cmg,ml->clg", extinction, upper, preferred_element_type=jnp.float32)
    ext32 = extinction.astype(jnp.float32)
    cosine = cosine_blk.astype(jnp.float32)
    lit_col = cosine > 0.0
    safe_cos = jnp.where(lit_col, cosine, jnp.float32(1.0))
    inverse = 1.0 / safe_cos
    downward = safe_cos[:, None, None] * jnp.exp(-above * inverse[:, None, None])
    absorbed = share * downward * (1.0 - jnp.exp(-ext32 * inverse[:, None, None]))
    heating = jnp.sum(absorbed * weights, axis=-1) * (levels / gpoints)
    bottom = safe_cos[:, None] * jnp.exp(-(above[:, -1, :] + ext32[:, -1, :]) * inverse[:, None])
    surface = jnp.sum(bottom * weights, axis=-1) / gpoints
    heating = jnp.where(lit_col[:, None], heating, jnp.float32(0.0))
    surface = jnp.where(lit_col, surface, jnp.float32(0.0))
    return (heating, surface)


def radiate(state_rows, cosine_rows, kcoef, scatter_coef, weights):
    total = state_rows.shape[0]
    block_count = total // block_cols
    state_blocks = state_rows.reshape(
        block_count, block_cols, state_rows.shape[1], state_rows.shape[2]
    )
    cosine_blocks = cosine_rows.reshape(block_count, block_cols)

    def one_block(pair):
        return column_optics(pair[0], pair[1], kcoef, scatter_coef, weights)

    heating, surface = lax.map(one_block, (state_blocks, cosine_blocks))
    return (heating.reshape(total, state_rows.shape[2]), surface.reshape(total))


def local(
    state,
    cosine_zenith,
    sunlit,
    kcoef,
    scatter_coef,
    gpoint_weight,
    sea_temp,
    intersection_col,
    intersection_weight,
    nearest_ocean,
):
    cosine_eff = cosine_zenith * sunlit.astype(jnp.bfloat16)
    columns = state.shape[0]
    levels = state.shape[2]
    atm_count = lax.axis_size("atm")
    own_index = lax.axis_index("atm")
    per_peer = columns // atm_count
    ranking = jnp.argsort(1 - sunlit, stable=True)
    target = jnp.arange(atm_count, dtype=jnp.int32)[:, None]
    within = jnp.arange(per_peer, dtype=jnp.int32)[None, :]
    position = (target - own_index) % atm_count + within * atm_count
    send_cols = ranking[position.reshape(-1)]
    outgoing = state[send_cols].reshape(atm_count, per_peer, state.shape[1], levels)
    out_cosine = cosine_eff[send_cols].reshape(atm_count, per_peer)
    incoming, in_cosine = (
        lax.all_to_all(outgoing, "atm", split_axis=0, concat_axis=0, tiled=True),
        lax.all_to_all(out_cosine, "atm", split_axis=0, concat_axis=0, tiled=True),
    )
    flat_cosine = in_cosine.reshape(-1)
    live_slot = (flat_cosine > 0).astype(jnp.int32)
    sun_count = columns // 2
    chosen = jnp.argsort(1 - live_slot, stable=True)[:sun_count]
    flat_state = incoming.reshape(columns, state.shape[1], levels)
    heat_rows, surf_rows = radiate(
        flat_state[chosen], flat_cosine[chosen], kcoef, scatter_coef, gpoint_weight
    )
    heat_slots = jnp.zeros((columns, levels), jnp.float32).at[chosen].set(heat_rows)
    surf_slots = jnp.zeros((columns,), jnp.float32).at[chosen].set(surf_rows)
    heat_back, surf_back = (
        lax.all_to_all(
            heat_slots.reshape(atm_count, per_peer, levels),
            "atm",
            split_axis=0,
            concat_axis=0,
            tiled=True,
        ),
        lax.all_to_all(
            surf_slots.reshape(atm_count, per_peer), "atm", split_axis=0, concat_axis=0, tiled=True
        ),
    )
    heating = (
        jnp.zeros((columns, levels), jnp.float32)
        .at[send_cols]
        .set(heat_back.reshape(columns, levels))
    )
    surface = jnp.zeros((columns,), jnp.float32).at[send_cols].set(surf_back.reshape(columns))
    section_flux = lax.all_gather(surface, "cpl", axis=0, tiled=True)
    picked = section_flux[intersection_col]
    weight_f = intersection_weight.astype(jnp.float32)
    ocean_flux = jnp.sum(weight_f * picked, axis=-1) / jnp.sum(weight_f, axis=-1)
    sea_next = relax_keep * sea_temp + forcing * ocean_flux
    section_sea = lax.all_gather(sea_next, "cpl", axis=0, tiled=True)
    column_sea = section_sea[nearest_ocean]
    return (heating, sea_next, column_sea)


def solution(mesh):
    return jax.shard_map(
        local,
        mesh=mesh,
        in_specs=(
            P(("atm", "cpl"), None, None),
            P(("atm", "cpl")),
            P(("atm", "cpl")),
            P(),
            P(),
            P(),
            P(("atm", "cpl")),
            P(("atm", "cpl"), None),
            P(("atm", "cpl"), None),
            P(("atm", "cpl")),
        ),
        out_specs=(P(("atm", "cpl"), None), P(("atm", "cpl")), P(("atm", "cpl"))),
        check_vma=False,
    )
```

profile of v0, /device:TPU:9, one launch (start us, length us, event | category | flops | bytes accessed | tf_op | source)
XLA Modules:
  0.0 290.7 jit_solution(3379579013737627324)
XLA Ops:
  1.5 3.8 %sort.31 = (s32[512]{0:T(512)}, s32[512]{0:T(512)S(1)}) sort(s32[512]{0:T(512)S(1)} %broadcast_subtract_fusion, s32[512]{0:T(512)S(1)} %iota.27), dimensions={0}, to_apply=%region_0.0 | sort | flops 4608 | bytes 8192 | tf_op jit(solution)/shard_map/jit(argsort)/sort | solution.py:75
  5.3 3.5 %gather_fusion = s32[512]{0:T(512)S(1)} fusion(s32[512]{0:T(512)S(1)} %get-tuple-element.48, s32[1024]{0:T(1024)S(1)} %pad_clamp_fusion.3), kind=kCustom, calls=%fused_computation | custom fusion | bytes 6144 | tf_op jit(solution)/shard_map/gather | solution.py:79
  9.5 3.5 %gather_fusion.1 = bf16[512]{0:T(512)(128)(2,1)S(1)} fusion(bf16[512]{0:T(512)(128)(2,1)S(1)} %convert_multiply_fusion, s32[1024]{0:T(1024)S(1)} %pad_clamp_fusion.2), kind=kCustom, calls=%fused_computation.1 | custom fusion | bytes 4096 | tf_op jit(solution)/shard_map/gather | solution.py:81
  13.7 5.7 %all-to-all-start = ((bf16[8,1,64]{2,1,0:T(2,128)(2,1)}), bf16[8,1,64]{2,1,0:T(2,128)(2,1)S(1)}, u32[]{:S(2)}, u32[]{:S(2)}) async-start(bf16[8,1,64]{2,1,0:T(2,128)(2,1)} %all_to_all.24), calls=%async_computation | async-start | bytes 8192 | tf_op jit(solution)/shard_map/all_to_all | solution.py:84
  19.4 5.4 %gather_fusion.3 = bf16[512,32,128]{2,1,0:T(8,128)(2,1)} fusion(bf16[512,32,128]{2,1,0:T(8,128)(2,1)} %param.12, s32[1024]{0:T(1024)S(1)} %pad_clamp_fusion.2), kind=kCustom, calls=%fused_computation.3 | custom fusion | bytes 8390656 | tf_op jit(solution)/shard_map/gather | solution.py:80
  24.8 5.6 %all-to-all-start.1 = ((bf16[8,64,32,128]{3,2,1,0:T(8,128)(2,1)}), bf16[8,64,32,128]{3,2,1,0:T(8,128)(2,1)}, u32[]{:S(2)}, u32[]{:S(2)}) async-start(bf16[8,64,32,128]{3,2,1,0:T(8,128)(2,1)} %bitcast.84), calls=%async_computation.1 | async-start | bytes 8388608 | tf_op jit(solution)/shard_map/all_to_all | solution.py:83
  30.8 3.8 %sort.32 = (s32[512]{0:T(512)}, s32[512]{0:T(512)S(1)}) sort(s32[512]{0:T(512)S(1)} %convert_subtract_fusion, s32[512]{0:T(512)S(1)} %iota.30), dimensions={0}, to_apply=%region_1.2 | sort | flops 4608 | bytes 8192 | tf_op jit(solution)/shard_map/jit(argsort)/sort | solution.py:89
  34.6 1.9 gather_fusion.2
  36.7 85.1 %all-to-all-done.1 = bf16[8,64,32,128]{3,2,1,0:T(8,128)(2,1)} async-done(((bf16[8,64,32,128]{3,2,1,0:T(8,128)(2,1)}), bf16[8,64,32,128]{3,2,1,0:T(8,128)(2,1)}, u32[]{:S(2)}, u32[]{:S(2)}) %all-to-all-start.1) | async-done | bytes 4194336 | tf_op jit(solution)/shard_map/all_to_all | solution.py:83
  121.8 3.2 %gather_fusion.4 = bf16[256,32,128]{2,1,0:T(8,128)(2,1)S(1)} fusion(bf16[512,32,128]{2,1,0:T(8,128)(2,1)} %bitcast.12, s32[1024]{0:T(1024)S(1)} %pad_clamp_fusion.1), kind=kCustom, calls=%fused_computation.4 | custom fusion | bytes 4195328 | tf_op jit(solution)/shard_map/gather | solution.py:92
  125.0 114.2 %while.12 = (s32[]{:T(128)}, f32[8,32,128]{2,1,0:T(8,128)S(1)}, f32[8,32]{1,0:T(8,128)S(1)}, bf16[8,32]{1,0:T(8,128)(2,1)S(1)}, bf16[8,32,32,128]{3,2,1,0:T(8,12...) while((s32[]{:T(128)}, f32[8,32,128]{2,1,0:T(8,128)S(1)}, ...), condition=%wide.region_5.6_spmd, body=%wide.region_2.5_spmd.sunk | while | flops 461377760 | bytes 26431960 | solution.py:53
  126.8 12.3 %fusion.35 = (f32[32,128,256]{2,1,0:T(8,128)S(1)}, f32[32,128]{1,0:T(8,128)S(1)}, f32[32,128,256]{2,1,0:T(8,128)S(1)}) fusion(f32[32,128,256]{2,1,0:T(8,128)S(1)} %get-tuple-element.141, u32[128,256]{1,0:T(8,128)S(1)} %get-tuple-element.142, f32[32,128,256]{2,1,0:T(8,128)S(1)} %get-tuple-element.143, u32[128,256]{1,0:T(8,128)S(1)} %get-tuple-element.144, ...), kind=kOutput, calls=%fused_computation.21.clone.1 | convolution fusion | flops 318779392 | bytes 17057024 | tf_op jit(solution)/shard_map/while/body/eval_jaxpr/cmg,ml->clg/dot_general | solution.py:26
  141.0 12.3 %fusion.35 = (f32[32,128,256]{2,1,0:T(8,128)S(1)}, f32[32,128]{1,0:T(8,128)S(1)}, f32[32,128,256]{2,1,0:T(8,128)S(1)}) fusion(f32[32,128,256]{2,1,0:T(8,128)S(1)} %get-tuple-element.141, u32[128,256]{1,0:T(8,128)S(1)} %get-tuple-element.142, f32[32,128,256]{2,1,0:T(8,128)S(1)} %get-tuple-element.143, u32[128,256]{1,0:T(8,128)S(1)} %get-tuple-element.144, ...), kind=kOutput, calls=%fused_computation.21.clone.1 | convolution fusion | flops 318779392 | bytes 17057024 | tf_op jit(solution)/shard_map/while/body/eval_jaxpr/cmg,ml->clg/dot_general | solution.py:26
  154.5 0.8 convert_reduce_fusion.6
  155.3 12.3 %fusion.35 = (f32[32,128,256]{2,1,0:T(8,128)S(1)}, f32[32,128]{1,0:T(8,128)S(1)}, f32[32,128,256]{2,1,0:T(8,128)S(1)}) fusion(f32[32,128,256]{2,1,0:T(8,128)S(1)} %get-tuple-element.141, u32[128,256]{1,0:T(8,128)S(1)} %get-tuple-element.142, f32[32,128,256]{2,1,0:T(8,128)S(1)} %get-tuple-element.143, u32[128,256]{1,0:T(8,128)S(1)} %get-tuple-element.144, ...), kind=kOutput, calls=%fused_computation.21.clone.1 | convolution fusion | flops 318779392 | bytes 17057024 | tf_op jit(solution)/shard_map/while/body/eval_jaxpr/cmg,ml->clg/dot_general | solution.py:26
  168.7 0.8 convert_reduce_fusion.6
  169.5 12.3 %fusion.35 = (f32[32,128,256]{2,1,0:T(8,128)S(1)}, f32[32,128]{1,0:T(8,128)S(1)}, f32[32,128,256]{2,1,0:T(8,128)S(1)}) fusion(f32[32,128,256]{2,1,0:T(8,128)S(1)} %get-tuple-element.141, u32[128,256]{1,0:T(8,128)S(1)} %get-tuple-element.142, f32[32,128,256]{2,1,0:T(8,128)S(1)} %get-tuple-element.143, u32[128,256]{1,0:T(8,128)S(1)} %get-tuple-element.144, ...), kind=kOutput, calls=%fused_computation.21.clone.1 | convolution fusion | flops 318779392 | bytes 17057024 | tf_op jit(solution)/shard_map/while/body/eval_jaxpr/cmg,ml->clg/dot_general | solution.py:26
  183.7 12.3 %fusion.35 = (f32[32,128,256]{2,1,0:T(8,128)S(1)}, f32[32,128]{1,0:T(8,128)S(1)}, f32[32,128,256]{2,1,0:T(8,128)S(1)}) fusion(f32[32,128,256]{2,1,0:T(8,128)S(1)} %get-tuple-element.141, u32[128,256]{1,0:T(8,128)S(1)} %get-tuple-element.142, f32[32,128,256]{2,1,0:T(8,128)S(1)} %get-tuple-element.143, u32[128,256]{1,0:T(8,128)S(1)} %get-tuple-element.144, ...), kind=kOutput, calls=%fused_computation.21.clone.1 | convolution fusion | flops 318779392 | bytes 17057024 | tf_op jit(solution)/shard_map/while/body/eval_jaxpr/cmg,ml->clg/dot_general | solution.py:26
  198.0 12.3 %fusion.35 = (f32[32,128,256]{2,1,0:T(8,128)S(1)}, f32[32,128]{1,0:T(8,128)S(1)}, f32[32,128,256]{2,1,0:T(8,128)S(1)}) fusion(f32[32,128,256]{2,1,0:T(8,128)S(1)} %get-tuple-element.141, u32[128,256]{1,0:T(8,128)S(1)} %get-tuple-element.142, f32[32,128,256]{2,1,0:T(8,128)S(1)} %get-tuple-element.143, u32[128,256]{1,0:T(8,128)S(1)} %get-tuple-element.144, ...), kind=kOutput, calls=%fused_computation.21.clone.1 | convolution fusion | flops 318779392 | bytes 17057024 | tf_op jit(solution)/shard_map/while/body/eval_jaxpr/cmg,ml->clg/dot_general | solution.py:26
  212.2 12.3 %fusion.35 = (f32[32,128,256]{2,1,0:T(8,128)S(1)}, f32[32,128]{1,0:T(8,128)S(1)}, f32[32,128,256]{2,1,0:T(8,128)S(1)}) fusion(f32[32,128,256]{2,1,0:T(8,128)S(1)} %get-tuple-element.141, u32[128,256]{1,0:T(8,128)S(1)} %get-tuple-element.142, f32[32,128,256]{2,1,0:T(8,128)S(1)} %get-tuple-element.143, u32[128,256]{1,0:T(8,128)S(1)} %get-tuple-element.144, ...), kind=kOutput, calls=%fused_computation.21.clone.1 | convolution fusion | flops 318779392 | bytes 17057024 | tf_op jit(solution)/shard_map/while/body/eval_jaxpr/cmg,ml->clg/dot_general | solution.py:26
  226.4 12.3 %fusion.35 = (f32[32,128,256]{2,1,0:T(8,128)S(1)}, f32[32,128]{1,0:T(8,128)S(1)}, f32[32,128,256]{2,1,0:T(8,128)S(1)}) fusion(f32[32,128,256]{2,1,0:T(8,128)S(1)} %get-tuple-element.141, u32[128,256]{1,0:T(8,128)S(1)} %get-tuple-element.142, f32[32,128,256]{2,1,0:T(8,128)S(1)} %get-tuple-element.143, u32[128,256]{1,0:T(8,128)S(1)} %get-tuple-element.144, ...), kind=kOutput, calls=%fused_computation.21.clone.1 | convolution fusion | flops 318779392 | bytes 17057024 | tf_op jit(solution)/shard_map/while/body/eval_jaxpr/cmg,ml->clg/dot_general | solution.py:26
  239.3 1.4 scatter_custom_fusion.2
  241.4 5.6 %all-to-all-start.3 = ((f32[8,1,64]{2,1,0:T(1,128)}), f32[8,1,64]{2,1,0:T(1,128)S(1)}, u32[]{:S(2)}, u32[]{:S(2)}) async-start(f32[8,1,64]{2,1,0:T(1,128)} %all_to_all.22), calls=%async_computation.3 | async-start | bytes 8192 | tf_op jit(solution)/shard_map/all_to_all | solution.py:104
  247.2 1.8 scatter_custom_fusion
  249.1 2.0 all-to-all-done.3
  251.0 4.7 %all-to-all-start.2 = ((f32[8,64,128]{2,1,0:T(8,128)}), f32[8,64,128]{2,1,0:T(8,128)S(1)}, u32[]{:S(2)}, u32[]{:S(2)}) async-start(f32[8,64,128]{2,1,0:T(8,128)} %bitcast.15), calls=%async_computation.2 | async-start | bytes 524288 | tf_op jit(solution)/shard_map/all_to_all | solution.py:97
  257.0 2.4 scatter_custom_fusion.3
  259.4 7.2 %all-gather = f32[4,1,512]{2,1,0:T(1,128)S(1)} all-gather(f32[1,1,512]{2,1,0:T(1,128)S(1)} %bitcast.87), channel_id=1, replica_groups=mesh['atm'=8,'cpl'=4] {'cpl'}, dimensions={0}, use_global_device_ids=true | all-gather | bytes 10240 | tf_op jit(solution)/shard_map/all_gather | solution.py:114
  266.6 11.8 %gather_fusion.5 = f32[2048]{0:T(1024)S(1)} fusion(f32[2048]{0:T(1024)S(1)} %bitcast.82, s32[2048]{0:T(1024)S(1)} %broadcast_clamp_fusion), kind=kCustom, calls=%fused_computation.5 | custom fusion | bytes 24576 | tf_op jit(solution)/shard_map/gather | solution.py:115
  278.9 5.2 %all-gather.1 = f32[4,1,512]{2,1,0:T(1,128)S(1)} all-gather(f32[1,1,512]{2,1,0:T(1,128)S(1)} %bitcast.92), channel_id=1, replica_groups=mesh['atm'=8,'cpl'=4] {'cpl'}, dimensions={0}, use_global_device_ids=true | all-gather | bytes 10240 | tf_op jit(solution)/shard_map/all_gather | solution.py:119
  284.0 4.3 %gather_fusion.6 = f32[512]{0:T(512)} fusion(f32[2048]{0:T(1024)S(1)} %bitcast.83, s32[1024]{0:T(1024)S(1)} %pad_clamp_fusion), kind=kCustom, calls=%fused_computation.6 | custom fusion | bytes 6144 | tf_op jit(solution)/shard_map/gather | solution.py:120
  288.3 2.4 scatter_custom_fusion.1
  (124 shorter events, 19.2 us)
Async XLA Ops:
  13.7 11.1 %all-to-all-start = ((bf16[8,1,64]{2,1,0:T(2,128)(2,1)}), bf16[8,1,64]{2,1,0:T(2,128)(2,1)S(1)}, u32[]{:S(2)}, u32[]{:S(2)}) async-start(bf16[8,1,64]{2,1,0:T(2,128)(2,1)} %all_to_all.24), calls=%async_computation | async-start | bytes 8192 | tf_op jit(solution)/shard_map/all_to_all | solution.py:84
  24.8 5.6 %copy-start.4 = (s32[512,4]{0,1:T(4,128)S(1)}, s32[512,4]{0,1:T(4,128)}, u32[]{:S(2)}) copy-start(s32[512,4]{0,1:T(4,128)} %param.19) | copy-start | bytes 24580
  24.8 97.0 %all-to-all-start.1 = ((bf16[8,64,32,128]{3,2,1,0:T(8,128)(2,1)}), bf16[8,64,32,128]{3,2,1,0:T(8,128)(2,1)}, u32[]{:S(2)}, u32[]{:S(2)}) async-start(bf16[8,64,32,128]{3,2,1,0:T(8,128)(2,1)} %bitcast.84), calls=%async_computation.1 | async-start | bytes 8388608 | tf_op jit(solution)/shard_map/all_to_all | solution.py:83
  30.3 94.7 %copy-start = (bf16[32,256]{1,0:T(8,128)(2,1)S(1)}, bf16[32,256]{1,0:T(8,128)(2,1)}, u32[]{:S(2)}) copy-start(bf16[32,256]{1,0:T(8,128)(2,1)} %param.15) | copy-start | bytes 49156
  30.3 94.7 %copy-start.1 = (bf16[32,256]{1,0:T(8,128)(2,1)S(1)}, bf16[32,256]{1,0:T(8,128)(2,1)}, u32[]{:S(2)}) copy-start(bf16[32,256]{1,0:T(8,128)(2,1)} %param.16) | copy-start | bytes 49156
  30.3 94.7 %copy-start.2 = (f32[256]{0:T(256)S(1)}, f32[256]{0:T(256)}, u32[]{:S(2)}) copy-start(f32[256]{0:T(256)} %param.17) | copy-start | bytes 3076
  125.0 122.0 %copy-start.6 = (s32[512]{0:T(512)S(1)}, s32[512]{0:T(512)}, u32[]{:S(2)}) copy-start(s32[512]{0:T(512)} %param.21) | copy-start | bytes 6148
  125.0 122.0 %copy-start.3 = (s32[512,4]{0,1:T(4,128)S(1)}, s32[512,4]{0,1:T(4,128)}, u32[]{:S(2)}) copy-start(s32[512,4]{0,1:T(4,128)} %param.20) | copy-start | bytes 24580
  241.4 9.6 %all-to-all-start.3 = ((f32[8,1,64]{2,1,0:T(1,128)}), f32[8,1,64]{2,1,0:T(1,128)S(1)}, u32[]{:S(2)}, u32[]{:S(2)}) async-start(f32[8,1,64]{2,1,0:T(1,128)} %all_to_all.22), calls=%async_computation.3 | async-start | bytes 8192 | tf_op jit(solution)/shard_map/all_to_all | solution.py:104
  251.0 37.3 %all-to-all-start.2 = ((f32[8,64,128]{2,1,0:T(8,128)}), f32[8,64,128]{2,1,0:T(8,128)S(1)}, u32[]{:S(2)}, u32[]{:S(2)}) async-start(f32[8,64,128]{2,1,0:T(8,128)} %bitcast.15), calls=%async_computation.2 | async-start | bytes 524288 | tf_op jit(solution)/shard_map/all_to_all | solution.py:97
  266.6 12.3 %copy-start.7 = (f32[512]{0:T(512)S(1)}, f32[512]{0:T(512)}, u32[]{:S(2)}) copy-start(f32[512]{0:T(512)} %param.18) | copy-start | bytes 6148
  278.9 11.8 %copy-start.5 = (f32[512]{0:T(512)}, f32[512]{0:T(512)S(1)}, u32[]{:S(2)}) copy-start(f32[512]{0:T(512)S(1)} %multiply_add_fusion) | copy-start | bytes 6148
where the time goes:
time: 292 us; the launch traced here: 291 us
  matrix products  110 us (38%)
  waiting for transfers between devices  87.1 us (30%)
  local copies, waits for them, and re-layouts  44.8 us (15%)
  starting transfers between devices  21.6 us (7%)
  other arithmetic  12.8 us (4%)
  blocking collectives  12.3 us (4%)
    dot_general x8, matrix products, column_optics(): jnp.einsum('cmg,ml->clg', extinction, upper, preferred_element_type=jnp.f...  98.3 us
    all_to_all x1, waiting for transfers between devices, local(): lax.all_to_all(outgoing, 'atm', split_axis=0, concat_axis=0, tiled=True)  85.1 us
    gather x2, local copies, waits for them, and re-layouts, local(): picked = section_flux[intersection_col]  12 us
    all_gather x1, blocking collectives, local(): section_flux = lax.all_gather(surface, 'cpl', axis=0, tiled=True)  7.17 us
    dot_general x8, matrix products, column_optics(): jnp.einsum('cfl,fg->clg', state_blk, kcoef, preferred_element_type=jnp.fl...  6.05 us
    dot_general x8, matrix products, column_optics(): jnp.einsum('cfl,fg->clg', state_blk, scatter_coef, preferred_element_type...  6.05 us
  transfers between devices with their start and end apart: 4, of which 2 were waited for; matrix products, arithmetic and copies ran while one was open for 12% of the time, Pallas kernels for 0%

commit v1 on v0

v1 whole, which is shorter than its diff:
```python
import functools

import jax
import jax.numpy as jnp
from jax import lax
from jax.experimental import pallas as pl
from jax.experimental.pallas import tpu as pltpu
from jax.sharding import PartitionSpec as P

depth_scale = 0.01
relax_keep = 0.75
forcing = 4.0
group_cols = 4
chunk_g = 64
log2e = 1.4426950408889634


def soft_plus(x):
    y = jnp.exp(jnp.minimum(x, 87.0))
    lifted = jnp.where(y < 1e-4, y - 0.5 * y * y, jnp.log(1.0 + y))
    return jnp.maximum(x, lifted)


def radiation_kernel(
    sunlit_ref, cosine_ref, state_ref, kabs_ref, ksca_ref, upper_ref, wide_ref, weight_ref,
    heat_ref, surf_ref, order_ref, ext_ref, part_ref,
):
    columns, levels = heat_ref.shape
    gpoints = kabs_ref.shape[0]
    heat_ref[...] = jnp.zeros_like(heat_ref)
    part_ref[...] = jnp.zeros_like(part_ref)

    def note(step, found):
        for inner in range(8):
            col = step * 8 + inner
            order_ref[found] = col
            found = found + sunlit_ref[col]
        return found

    count = lax.fori_loop(0, columns // 8, note, jnp.int32(0))
    row_id = lax.broadcasted_iota(jnp.int32, (8, 2 * levels), 0)
    lane_id = lax.broadcasted_iota(jnp.int32, (8, 2 * levels), 1)
    select = ((lane_id // levels) == row_id).astype(jnp.bfloat16)
    row8 = lax.broadcasted_iota(jnp.int32, (8, gpoints), 0)
    lane1 = lax.broadcasted_iota(jnp.int32, (1, 2 * levels), 1)

    def group(step, carry):
        for pair in range(group_cols // 2):
            base = step * group_cols + 2 * pair
            first, second = order_ref[base], order_ref[base + 1]
            u_first, u_second = cosine_ref[first], cosine_ref[second]
            u_lane = jnp.where(lane1 < levels, u_first, u_second)
            rate = -1.0 / u_lane
            both = jnp.concatenate([state_ref[first], state_ref[second]], axis=1)
            total = jnp.zeros((8, 2 * levels), jnp.float32)
            for low in range(0, gpoints, chunk_g):
                rows = slice(low, low + chunk_g)
                soft_abs = soft_plus(
                    jnp.dot(kabs_ref[rows], both, preferred_element_type=jnp.float32)
                )
                soft_sca = soft_plus(
                    jnp.dot(ksca_ref[rows], both, preferred_element_type=jnp.float32)
                )
                soft = soft_abs + soft_sca
                ext = (depth_scale * soft).astype(jnp.bfloat16)
                ext_ref[pair, rows] = ext
                above = jnp.dot(ext, upper_ref[...], preferred_element_type=jnp.float32)
                reach = jnp.exp(above * rate - jnp.log(soft))
                lost = 1.0 - jnp.exp(ext.astype(jnp.float32) * rate)
                term = soft_abs * reach * (lost * wide_ref[rows])
                total = total + jnp.sum(term.reshape(chunk_g // 8, 8, 2 * levels), axis=0)
            row = jnp.sum(total, axis=0, keepdims=True) * (u_lane * (levels / gpoints))
            heat_ref[pl.ds(first, 1), :] = row[:, :levels]
            heat_ref[pl.ds(second, 1), :] = row[:, levels:]
            depth = lax.dot_general(
                select, ext_ref[pair], (((1,), (1,)), ((), ())),
                preferred_element_type=jnp.float32,
            )
            u_row = jnp.where(row8 == 0, u_first, u_second)
            bottom = u_row * jnp.exp(-depth / u_row) * (weight_ref[...] / gpoints)
            half = bottom[:, : gpoints // 2] + bottom[:, gpoints // 2 :]
            part_ref[pl.ds(first, 1), :] = half[0:1]
            part_ref[pl.ds(second, 1), :] = half[1:2]
        return carry

    lax.fori_loop(0, count // group_cols, group, jnp.int32(0))
    surf_ref[...] = jnp.sum(part_ref[...].reshape(columns // 128, 128, 128), axis=-1)


def radiation(sunlit, cosine, state, kcoef, scatter_coef, weights):
    columns, feats, levels = state.shape
    gpoints = kcoef.shape[1]
    row_index = lax.broadcasted_iota(jnp.int32, (2 * levels, 2 * levels), 0)
    col_index = lax.broadcasted_iota(jnp.int32, (2 * levels, 2 * levels), 1)
    same = (row_index // levels) == (col_index // levels)
    upper = (same & (row_index < col_index)).astype(jnp.bfloat16)
    wide = jnp.broadcast_to(weights[:, None], (gpoints, 2 * levels))
    vmem = pl.BlockSpec(memory_space=pltpu.VMEM)
    smem = pl.BlockSpec(memory_space=pltpu.SMEM)
    return pl.pallas_call(
        radiation_kernel,
        out_shape=(
            jax.ShapeDtypeStruct((columns, levels), jnp.float32),
            jax.ShapeDtypeStruct((columns // 128, 128), jnp.float32),
        ),
        in_specs=[smem, smem, vmem, vmem, vmem, vmem, vmem, vmem],
        out_specs=(vmem, vmem),
        scratch_shapes=[
            pltpu.SMEM((columns + 8,), jnp.int32),
            pltpu.VMEM((group_cols // 2, gpoints, 2 * levels), jnp.bfloat16),
            pltpu.VMEM((columns, 128), jnp.float32),
        ],
        compiler_params=pltpu.CompilerParams(vmem_limit_bytes=40 * 1024 * 1024),
        name="radiation",
    )(sunlit, cosine, state, kcoef.T, scatter_coef.T, upper, wide, weights[None, :])


def pick(table, index):
    low = index % 128
    high = index // 128
    found = jnp.zeros(index.shape, jnp.float32)
    for row in range(table.shape[0]):
        line = jnp.broadcast_to(table[row : row + 1], index.shape)
        found = jnp.where(high == row, jnp.take_along_axis(line, low, axis=1), found)
    return found


def ocean_kernel(flux_ref, icol_ref, iweight_ref, sea_ref, next_ref):
    picked = pick(flux_ref[...], icol_ref[...])
    weight = iweight_ref[...].astype(jnp.float32)
    product = weight * picked
    rows = sea_ref.shape[0]
    overlaps = weight.shape[0] // rows
    top = product[:rows]
    bottom = weight[:rows]
    for k in range(1, overlaps):
        top = top + product[k * rows : (k + 1) * rows]
        bottom = bottom + weight[k * rows : (k + 1) * rows]
    next_ref[...] = relax_keep * sea_ref[...] + forcing * (top / bottom)


def column_kernel(sea_ref, near_ref, out_ref):
    out_ref[...] = pick(sea_ref[...], near_ref[...])


def local(
    state, cosine_zenith, sunlit, kcoef, scatter_coef, gpoint_weight, sea_temp,
    intersection_col, intersection_weight, nearest_ocean,
):
    cosine = cosine_zenith.astype(jnp.float32)
    cells = sea_temp.shape[0]
    heating, surface = radiation(sunlit, cosine, state, kcoef, scatter_coef, gpoint_weight)
    icol = intersection_col.T.reshape(-1, 128)
    iweight = intersection_weight.T.reshape(-1, 128)
    section_flux = lax.all_gather(surface, "cpl", axis=0, tiled=True)
    sea_next = pl.pallas_call(
        ocean_kernel,
        out_shape=jax.ShapeDtypeStruct((cells // 128, 128), jnp.float32),
        name="ocean",
    )(section_flux, icol, iweight, sea_temp.reshape(-1, 128))
    section_sea = lax.all_gather(sea_next, "cpl", axis=0, tiled=True)
    column_sea = pl.pallas_call(
        column_kernel,
        out_shape=jax.ShapeDtypeStruct((nearest_ocean.shape[0] // 128, 128), jnp.float32),
        name="column",
    )(section_sea, nearest_ocean.reshape(-1, 128))
    return (heating, sea_next.reshape(-1), column_sea.reshape(-1))


def solution(mesh):
    both = ("atm", "cpl")
    return jax.shard_map(
        local,
        mesh=mesh,
        in_specs=(
            P(both, None, None), P(both), P(both), P(), P(), P(), P(both),
            P(both, None), P(both, None), P(both),
        ),
        out_specs=(P(both, None), P(both), P(both)),
        check_vma=False,
    )
```

time: 292 us -> 161 us (0.55)
  Pallas kernels: 0 us -> 139 us
  matrix products: 110 us -> 0 us
  waiting for transfers between devices: 87.1 us -> 0 us
  local copies, waits for them, and re-layouts: 44.8 us -> 7.21 us
  starting transfers between devices: 21.6 us -> 0 us
  other arithmetic: 12.8 us -> 0.87 us
    pallas_call x0 -> x3, Pallas kernels: none -> 139 us  [the longest x1 136 us: radiation(): pl.pallas_call(radiation_kernel, out_shape=(jax.ShapeDtypeStruct((columns...]
    dot_general x24 -> x0, matrix products: 110 us -> none  [the longest x8 98.3 us: column_optics(): jnp.einsum('cmg,ml->clg', extinction, upper, preferred_element_type=jnp.f...]
    all_to_all x4 -> x0, waiting for transfers between devices: 87.1 us -> none  [the longest x1 85.1 us: local(): lax.all_to_all(outgoing, 'atm', split_axis=0, concat_axis=0, tiled=True)]
    gather x8 -> x0, local copies, waits for them, and re-layouts: 33.8 us -> none  [the longest x2 12 us: local(): picked = section_flux[intersection_col]]
    all_to_all x4 -> x0, starting transfers between devices: 21.6 us -> none  [the longest x1 5.69 us: local(): lax.all_to_all(out_cosine, 'atm', split_axis=0, concat_axis=0, tiled=True)]
    scatter x4 -> x0, local copies, waits for them, and re-layouts: 8.02 us -> none  [the longest x1 2.43 us: local(): jnp.zeros((columns,), jnp.float32).at[send_cols]]
    sort x2 -> x0, other arithmetic: 7.54 us -> none  [the longest x1 3.77 us: local(): chosen = jnp.argsort(1 - live_slot, stable=True)[:sun_count]]
    unnamed x17 -> x12, local copies, waits for them, and re-layouts: 0.18 us -> 5.23 us
  transfers between devices with their start and end apart: 4 -> 0, of which waited for: 2 -> 0; matrix products, arithmetic and copies ran while one was open for 12% -> 0% of each run, Pallas kernels for 0% -> 0%
where the time goes in v1:
time: 161 us; the launch traced here: 160 us
  Pallas kernels  139 us (86%)
  blocking collectives  12.6 us (8%)
  local copies, waits for them, and re-layouts  7.21 us (4%)
    pallas_call x1, Pallas kernels, radiation(): pl.pallas_call(radiation_kernel, out_shape=(jax.ShapeDtypeStruct((columns...  136 us
    all_gather x1, blocking collectives, local(): section_sea = lax.all_gather(sea_next, 'cpl', axis=0, tiled=True)  7.02 us
    all_gather x1, blocking collectives, local(): section_flux = lax.all_gather(surface, 'cpl', axis=0, tiled=True)  5.6 us
    unnamed x12, local copies, waits for them, and re-layouts  5.23 us

profile of v1, /device:TPU:9, one launch (start us, length us, event | category | flops | bytes accessed | tf_op | source)
XLA Modules:
  0.0 160.0 jit_solution(4922301148508556614)
XLA Ops:
  0.6 0.0 copy-start.3
  0.6 0.0 copy-start.4
  0.7 0.2 fusion.1.upper_ref
  0.9 0.8 broadcast_in_dim.4.wide_ref
  1.6 0.8 copy.15
  2.5 0.8 copy.16
  3.3 0.7 convert_element_type.6.cosine_ref
  4.0 0.0 copy-start
  4.0 2.2 %copy-done = bf16[512,32,128]{2,1,0:T(8,128)(2,1)S(1)} copy-done((bf16[512,32,128]{2,1,0:T(8,128)(2,1)S(1)}, bf16[512,32,128]{2,1,0:T(8,128)(2,1)}, u32[]{:S(2)}) %copy-start) | copy-done | bytes 4194328
  6.2 0.0 copy-start.1
  6.2 0.7 copy-done.1
  6.9 0.0 copy-start.2
  6.9 0.7 copy-done.2
  7.5 135.8 %radiation.1 = (f32[512,128]{1,0:T(8,128)}, f32[4,128]{1,0:T(4,128)S(1)}) custom-call(s32[512]{0:T(512)S(1)} %copy-done.2, f32[512]{0:T(512)S(1)} %convert_element_type.6.cosine_ref, bf16[512,32,128]{2,1,0:T(8,128)(2,1)S(1)} %copy-done, bf16[256,32]{1,0:T(8,128)(2,1)S(1)} %bitcast.13, bf16[256,32]{1,0:T(8,128)(2,1)S(1)} %bitcast.14, ...), custom_call_target="tpu_custom_call" | custom-call | tf_op jit(solution)/shard_map/radiation/pallas_call | solution.py:100
  143.3 5.6 %all-gather = f32[4,4,128]{2,1,0:T(4,128)} all-gather(f32[1,4,128]{2,1,0:T(4,128)S(1)} %bitcast.16), channel_id=1, replica_groups=mesh['atm'=8,'cpl'=4] {'cpl'}, dimensions={0}, use_global_device_ids=true | all-gather | bytes 10240 | tf_op jit(solution)/shard_map/all_gather | solution.py:155
  148.9 0.0 copy-done.3
  148.9 0.6 reshape.25.icol_ref
  149.5 0.0 copy-done.4
  149.5 0.6 reshape.26.iweight_ref
  150.1 1.4 ocean.1
  151.6 7.0 %all-gather.1 = f32[4,4,128]{2,1,0:T(4,128)} all-gather(f32[1,4,128]{2,1,0:T(4,128)} %bitcast.19), channel_id=1, replica_groups=mesh['atm'=8,'cpl'=4] {'cpl'}, dimensions={0}, use_global_device_ids=true | all-gather | bytes 10240 | tf_op jit(solution)/shard_map/all_gather | solution.py:161
  158.6 1.4 column.1
  (2 shorter events, 0.0 us)
Async XLA Ops:
  0.6 148.3 %copy-start.3 = (s32[512,4]{0,1:T(4,128)S(1)}, s32[512,4]{0,1:T(4,128)}, u32[]{:S(2)}) copy-start(s32[512,4]{0,1:T(4,128)} %param.17) | copy-start | bytes 24580
  0.6 148.9 %copy-start.4 = (s32[512,4]{0,1:T(4,128)S(1)}, s32[512,4]{0,1:T(4,128)}, u32[]{:S(2)}) copy-start(s32[512,4]{0,1:T(4,128)} %param.18) | copy-start | bytes 24580
  4.0 2.2 %copy-start = (bf16[512,32,128]{2,1,0:T(8,128)(2,1)S(1)}, bf16[512,32,128]{2,1,0:T(8,128)(2,1)}, u32[]{:S(2)}) copy-start(bf16[512,32,128]{2,1,0:T(8,128)(2,1)} %state_ref.1) | copy-start | bytes 12582916
  6.2 0.7 copy-start.1
  6.9 0.7 copy-start.2

commit v2 on v1

--- a/solution.py
+++ b/solution.py
@@ -10,25 +10,22 @@
 depth_scale = 0.01
 relax_keep = 0.75
 forcing = 4.0
-group_cols = 4
+group_cols = 8
+moved_cols = 144
 chunk_g = 64
 log2e = 1.4426950408889634
-
-
-def soft_plus(x):
-    y = jnp.exp(jnp.minimum(x, 87.0))
-    lifted = jnp.where(y < 1e-4, y - 0.5 * y * y, jnp.log(1.0 + y))
-    return jnp.maximum(x, lifted)
-
-
-def radiation_kernel(
-    sunlit_ref, cosine_ref, state_ref, kabs_ref, ksca_ref, upper_ref, wide_ref, weight_ref,
-    heat_ref, surf_ref, order_ref, ext_ref, part_ref,
-):
-    columns, levels = heat_ref.shape
-    gpoints = kabs_ref.shape[0]
-    heat_ref[...] = jnp.zeros_like(heat_ref)
-    part_ref[...] = jnp.zeros_like(part_ref)
+ln2 = 0.6931471805599453
+
+
+def soft_plus2(t):
+    y = jnp.exp2(jnp.minimum(t, 126.0))
+    lifted = jnp.where(y < 1e-4, y * (log2e - (0.5 * log2e) * y), lax.log2(1.0 + y))
+    return jnp.maximum(t, lifted)
+
+
+def pack_kernel(sunlit_ref, cosine_ref, state_ref, packed_ref, sent_ref, order_ref, meta_ref):
+    columns = state_ref.shape[0]
+    moved = packed_ref.shape[0]
 
     def note(step, found):
         for inner in range(8):
@@ -38,10 +35,60 @@
         return found
 
     count = lax.fori_loop(0, columns // 8, note, jnp.int32(0))
+    excess = jnp.clip(count - columns // 2, 0, moved)
+    base = count - excess
+    meta_ref[0] = base
+    meta_ref[1] = excess
+
+    def copy(step, carry):
+        for inner in range(8):
+            slot = step * 8 + inner
+            col = order_ref[base + slot]
+            packed_ref[slot] = state_ref[col]
+            sent_ref[slot] = cosine_ref[col]
+        return carry
+
+    def blank(slot, carry):
+        sent_ref[slot] = jnp.float32(0.0)
+        return carry
+
+    lax.fori_loop(0, excess // 8, copy, jnp.int32(0))
+    lax.fori_loop(excess, moved, blank, jnp.int32(0))
+
+
+def merge_kernel(order_ref, meta_ref, surf_in_ref, heat_in_ref, part_in_ref, back_ref, heat_ref, surf_ref, part_ref):
+    heat_ref[...] = heat_in_ref[...]
+    part_ref[...] = part_in_ref[...]
+    base, excess = meta_ref[0], meta_ref[1]
+    lane = lax.broadcasted_iota(jnp.int32, (1, 128), 1)
+
+    def put(step, carry):
+        for inner in range(8):
+            slot = step * 8 + inner
+            col = order_ref[base + slot]
+            heat_ref[pl.ds(col, 1), :] = back_ref[pl.ds(slot, 1), :]
+            part_ref[pl.ds(col, 1), :] = jnp.where(lane == 0, surf_in_ref[slot], 0.0)
+        return carry
+
+    lax.fori_loop(0, excess // 8, put, jnp.int32(0))
+    columns = heat_ref.shape[0]
+    surf_ref[...] = jnp.sum(part_ref[...].reshape(columns // 128, 128, 128), axis=-1)
+
+
+def radiation_kernel(
+    order_ref, count_ref, cosine_ref, state_ref, kabs_ref, ksca_ref, upper_ref, wide_ref, weight_ref,
+    heat_ref, part_ref, ext_ref,
+):
+    columns, levels = heat_ref.shape
+    gpoints = kabs_ref.shape[0]
+    heat_ref[...] = jnp.zeros_like(heat_ref)
+    part_ref[...] = jnp.zeros_like(part_ref)
+    count = count_ref[0]
     row_id = lax.broadcasted_iota(jnp.int32, (8, 2 * levels), 0)
     lane_id = lax.broadcasted_iota(jnp.int32, (8, 2 * levels), 1)
     select = ((lane_id // levels) == row_id).astype(jnp.bfloat16)
     row8 = lax.broadcasted_iota(jnp.int32, (8, gpoints), 0)
+    start = lax.broadcasted_iota(jnp.int32, (chunk_g, 2 * levels), 1) % levels == 0
     lane1 = lax.broadcasted_iota(jnp.int32, (1, 2 * levels), 1)
 
     def group(step, carry):
@@ -50,24 +97,26 @@
             first, second = order_ref[base], order_ref[base + 1]
             u_first, u_second = cosine_ref[first], cosine_ref[second]
             u_lane = jnp.where(lane1 < levels, u_first, u_second)
-            rate = -1.0 / u_lane
+            rate = -log2e / u_lane
             both = jnp.concatenate([state_ref[first], state_ref[second]], axis=1)
+            both = jnp.concatenate([both, both, both], axis=0)
             total = jnp.zeros((8, 2 * levels), jnp.float32)
             for low in range(0, gpoints, chunk_g):
                 rows = slice(low, low + chunk_g)
-                soft_abs = soft_plus(
+                soft_abs = soft_plus2(
                     jnp.dot(kabs_ref[rows], both, preferred_element_type=jnp.float32)
                 )
-                soft_sca = soft_plus(
+                soft_sca = soft_plus2(
                     jnp.dot(ksca_ref[rows], both, preferred_element_type=jnp.float32)
                 )
                 soft = soft_abs + soft_sca
-                ext = (depth_scale * soft).astype(jnp.bfloat16)
+                ext = ((depth_scale * ln2) * soft).astype(jnp.bfloat16)
                 ext_ref[pair, rows] = ext
-                above = jnp.dot(ext, upper_ref[...], preferred_element_type=jnp.float32)
-                reach = jnp.exp(above * rate - jnp.log(soft))
-                lost = 1.0 - jnp.exp(ext.astype(jnp.float32) * rate)
-                term = soft_abs * reach * (lost * wide_ref[rows])
+                through = jnp.dot(ext, upper_ref[...], preferred_element_type=jnp.float32)
+                leave = jnp.exp2(through * rate)
+                enter = jnp.where(start, 1.0, pltpu.roll(leave, 1, 1))
+                share = soft_abs * pl.reciprocal(soft, approx=False)
+                term = share * (enter - leave) * wide_ref[rows]
                 total = total + jnp.sum(term.reshape(chunk_g // 8, 8, 2 * levels), axis=0)
             row = jnp.sum(total, axis=0, keepdims=True) * (u_lane * (levels / gpoints))
             heat_ref[pl.ds(first, 1), :] = row[:, :levels]
@@ -84,35 +133,102 @@
         return carry
 
     lax.fori_loop(0, count // group_cols, group, jnp.int32(0))
-    surf_ref[...] = jnp.sum(part_ref[...].reshape(columns // 128, 128, 128), axis=-1)
-
-
-def radiation(sunlit, cosine, state, kcoef, scatter_coef, weights):
-    columns, feats, levels = state.shape
-    gpoints = kcoef.shape[1]
+
+
+def split_terms(coef):
+    scaled = coef.T.astype(jnp.float32) * log2e
+    high = lax.reduce_precision(scaled, 8, 7)
+    middle = lax.reduce_precision(scaled - high, 8, 7)
+    low = scaled - high - middle
+    return jnp.concatenate([high, middle, low], axis=1).astype(jnp.bfloat16)
+
+
+def tables(kcoef, scatter_coef, weights, levels):
     row_index = lax.broadcasted_iota(jnp.int32, (2 * levels, 2 * levels), 0)
     col_index = lax.broadcasted_iota(jnp.int32, (2 * levels, 2 * levels), 1)
     same = (row_index // levels) == (col_index // levels)
-    upper = (same & (row_index < col_index)).astype(jnp.bfloat16)
-    wide = jnp.broadcast_to(weights[:, None], (gpoints, 2 * levels))
-    vmem = pl.BlockSpec(memory_space=pltpu.VMEM)
-    smem = pl.BlockSpec(memory_space=pltpu.SMEM)
+    upper = (same & (row_index <= col_index)).astype(jnp.bfloat16)
+    wide = jnp.broadcast_to(weights[:, None], (weights.shape[0], 2 * levels))
+    return split_terms(kcoef), split_terms(scatter_coef), upper, wide, weights[None, :]
+
+
+vmem = pl.BlockSpec(memory_space=pltpu.VMEM)
+smem = pl.BlockSpec(memory_space=pltpu.SMEM)
+
+
+def pack(sunlit, cosine, state, moved):
+    columns, feats, levels = state.shape
+    return pl.pallas_call(
+        pack_kernel,
+        out_shape=(
+            jax.ShapeDtypeStruct((moved, feats, levels), state.dtype),
+            jax.ShapeDtypeStruct((moved,), jnp.float32),
+            jax.ShapeDtypeStruct((columns + 8,), jnp.int32),
+            jax.ShapeDtypeStruct((8,), jnp.int32),
+        ),
+        in_specs=[smem, smem, vmem],
+        out_specs=(vmem, smem, smem, smem),
+        compiler_params=pltpu.CompilerParams(vmem_limit_bytes=16 * 1024 * 1024),
+        name="pack",
+    )(sunlit, cosine, state)
+
+
+def radiation(order, count, cosine, state, constants):
+    columns, feats, levels = state.shape
+    gpoints = constants[0].shape[0]
     return pl.pallas_call(
         radiation_kernel,
         out_shape=(
             jax.ShapeDtypeStruct((columns, levels), jnp.float32),
-            jax.ShapeDtypeStruct((columns // 128, 128), jnp.float32),
-        ),
-        in_specs=[smem, smem, vmem, vmem, vmem, vmem, vmem, vmem],
+            jax.ShapeDtypeStruct((columns, 128), jnp.float32),
+        ),
+        in_specs=[smem, smem, smem, vmem, vmem, vmem, vmem, vmem, vmem],
         out_specs=(vmem, vmem),
         scratch_shapes=[
-            pltpu.SMEM((columns + 8,), jnp.int32),
             pltpu.VMEM((group_cols // 2, gpoints, 2 * levels), jnp.bfloat16),
-            pltpu.VMEM((columns, 128), jnp.float32),
         ],
-        compiler_params=pltpu.CompilerParams(vmem_limit_bytes=40 * 1024 * 1024),
+        compiler_params=pltpu.CompilerParams(vmem_limit_bytes=24 * 1024 * 1024),
+        cost_estimate=pl.CostEstimate(
+            flops=columns * levels * gpoints * 1000,
+            bytes_accessed=columns * feats * levels * 2,
+            transcendentals=columns * levels * gpoints * 6,
+        ),
         name="radiation",
-    )(sunlit, cosine, state, kcoef.T, scatter_coef.T, upper, wide, weights[None, :])
+    )(order, count, cosine, state, *constants)
+
+
+def merge(order, meta, surf_back, heat, part, back):
+    columns, levels = heat.shape
+    return pl.pallas_call(
+        merge_kernel,
+        out_shape=(
+            jax.ShapeDtypeStruct((columns, levels), jnp.float32),
+            jax.ShapeDtypeStruct((columns // 128, 128), jnp.float32),
+        ),
+        in_specs=[smem, smem, smem, vmem, vmem, vmem],
+        out_specs=(vmem, vmem),
+        scratch_shapes=[pltpu.VMEM((columns, 128), jnp.float32)],
+        name="merge",
+    )(order, meta, surf_back, heat, part, back)
+
+
+def balanced(sunlit, cosine, state, kcoef, scatter_coef, weights):
+    levels = state.shape[2]
+    atm_count = lax.axis_size("atm")
+    swap = [(i, (i + atm_count // 2) % atm_count) for i in range(atm_count)]
+    constants = tables(kcoef, scatter_coef, weights, levels)
+    packed, sent, order, meta = pack(sunlit, cosine, state, moved_cols)
+    guest = lax.ppermute(packed, "atm", swap)
+    guest_cosine = lax.ppermute(sent, "atm", swap)
+    heat, part = radiation(order, meta, cosine, state, constants)
+    guest_count = jnp.sum((guest_cosine > 0).astype(jnp.int32)).reshape(1)
+    guest_heat, guest_part = radiation(
+        jnp.arange(moved_cols, dtype=jnp.int32), guest_count, guest_cosine, guest, constants
+    )
+    guest_surf = jnp.sum(guest_part, axis=-1)
+    back = lax.ppermute(guest_heat, "atm", swap)
+    surf_back = lax.ppermute(guest_surf, "atm", swap)
+    return merge(order, meta, surf_back, heat, part, back)
 
 
 def pick(table, index):
@@ -149,7 +265,7 @@
 ):
     cosine = cosine_zenith.astype(jnp.float32)
     cells = sea_temp.shape[0]
-    heating, surface = radiation(sunlit, cosine, state, kcoef, scatter_coef, gpoint_weight)
+    heating, surface = balanced(sunlit, cosine, state, kcoef, scatter_coef, gpoint_weight)
     icol = intersection_col.T.reshape(-1, 128)
     iweight = intersection_weight.T.reshape(-1, 128)
     section_flux = lax.all_gather(surface, "cpl", axis=0, tiled=True)

time: 161 us -> 222 us (1.38)
  blocking collectives: 12.6 us -> 110 us
  Pallas kernels: 139 us -> 46.6 us
  waiting for transfers between devices: 0 us -> 49.5 us
  starting transfers between devices: 0 us -> 4.85 us
    all_gather x1, blocking collectives: 5.6 us -> 104 us  [local(): section_flux = lax.all_gather(surface, 'cpl', axis=0, tiled=True)]
    pallas_call x1 -> x2, Pallas kernels: 136 us -> 38.9 us  [radiation(): pl.pallas_call(radiation_kernel, out_shape=(jax.ShapeDtypeStruct((columns...]
    ppermute x0 -> x4, waiting for transfers between devices: none -> 49.5 us  [the longest x1 49.5 us: balanced(): guest_cosine = lax.ppermute(sent, 'atm', swap)]
    ppermute x0 -> x4, starting transfers between devices: none -> 4.85 us  [the longest x1 2.35 us: balanced(): back = lax.ppermute(guest_heat, 'atm', swap)]
    pallas_call x0 -> x2, Pallas kernels: none -> 4.85 us  [the longest x1 3.04 us: pack(): pl.pallas_call(pack_kernel, out_shape=(jax.ShapeDtypeStruct((moved, feats...]
    unnamed x12 -> x28, local copies, waits for them, and re-layouts: 5.23 us -> 7.09 us
  transfers between devices with their start and end apart: 0 -> 4, of which waited for: 0 -> 1; matrix products, arithmetic and copies ran while one was open for 0% -> 1% of each run, Pallas kernels for 0% -> 0%
where the time goes in v2:
time: 222 us
  blocking collectives  110 us (50%)
  waiting for transfers between devices  49.5 us (22%)
  Pallas kernels  46.6 us (21%)
  local copies, waits for them, and re-layouts  8.6 us (4%)
  starting transfers between devices  4.85 us (2%)
    all_gather x1, blocking collectives, local(): section_flux = lax.all_gather(surface, 'cpl', axis=0, tiled=True)  104 us
    ppermute x1, waiting for transfers between devices, balanced(): guest_cosine = lax.ppermute(sent, 'atm', swap)  49.5 us
    pallas_call x2, Pallas kernels, radiation(): pl.pallas_call(radiation_kernel, out_shape=(jax.ShapeDtypeStruct((columns...  38.9 us
    unnamed x28, local copies, waits for them, and re-layouts  7.09 us
    all_gather x1, blocking collectives, local(): section_sea = lax.all_gather(sea_next, 'cpl', axis=0, tiled=True)  5.81 us
  transfers between devices with their start and end apart: 4, of which 1 were waited for; matrix products, arithmetic and copies ran while one was open for 1% of the time, Pallas kernels for 0%

profile of v2, /device:TPU:9, one launch (start us, length us, event | category | flops | bytes accessed | tf_op | source)
XLA Modules:
  0.0 221.8 jit_solution(10932269161757040277)
XLA Ops:
  0.6 0.7 convert_element_type.21.cosine_ref
  1.3 2.2 copy-done
  3.5 0.7 copy-done.5
  4.2 3.0 %pack.1 = (bf16[144,32,128]{2,1,0:T(8,128)(2,1)S(1)}, f32[144]{0:T(256)S(1)}, s32[520]{0:T(1024)S(1)}, s32[8]{0:T(128)S(1)}) custom-call(s32[512]{0:T(512)S(1)} %copy-done.5, f32[512]{0:T(512)S(1)} %convert_element_type.21.cosine_ref, bf16[512,32,128]{2,1,0:T(8,128)(2,1)S(1)} %copy-done), custom_call_target="tpu_custom_call" | custom-call | tf_op jit(solution)/shard_map/pack/pallas_call | solution.py:161
  7.3 0.0 copy-start.6
  7.3 1.9 collective-permute-start.1
  9.2 0.5 collective-permute-start
  9.7 0.1 copy.17
  9.8 0.1 copy.18
  9.9 0.2 fusion.1.upper_ref
  10.2 0.1 pad_maximum_fusion
  10.4 49.5 %collective-permute-done.cosine_ref = f32[144]{0:T(256)S(1)} collective-permute-done((f32[144]{0:T(256)S(1)}, f32[144]{0:T(256)S(1)}, u32[]{:S(2)}, u32[]{:S(2)}) %collective-permute-start) | collective-permute-done | bytes 608 | tf_op jit(solution)/shard_map/ppermute | solution.py:222
  59.8 0.6 fusion.4
  60.5 0.0 collective-permute-done.1.state_ref
  60.5 0.1 broadcast_in_dim.4.wide_ref
  60.6 38.3 %radiation.2 = (f32[144,128]{1,0:T(8,128)S(1)}, f32[144,128]{1,0:T(8,128)S(1)}) custom-call(s32[144]{0:T(256)S(1)} %iota.45.order_ref, s32[1]{0:T(128)} %bitcast.count_ref, f32[144]{0:T(256)S(1)} %collective-permute-done.cosine_ref, bf16[144,32,128]{2,1,0:T(8,128)(2,1)S(1)} %collective-permute-done.1.state_ref, ...), custom_call_target="tpu_custom_call" | custom-call | flops 4718592000 | bytes 1179648 | tf_op jit(solution)/shard_map/radiation/pallas_call | solution.py:179
  98.9 0.1 reduce_sum.19
  99.0 0.1 collective-permute-start.2
  99.1 2.4 %collective-permute-start.3 = (f32[144,128]{1,0:T(8,128)S(1)}, f32[144,128]{1,0:T(8,128)S(1)}, u32[]{:S(2)}, u32[]{:S(2)}) collective-permute-start(f32[144,128]{1,0:T(8,128)S(1)} %get-tuple-element.20), channel_id=1, source_target_pairs={{0,16},{4,20},{8,24},{12,28},{16,0},{20,4},{24,8},{28,12},{1,17},{... | collective-permute-start | bytes 221192 | tf_op jit(solution)/shard_map/ppermute | solution.py:229
  101.4 2.2 copy-done.1
  103.6 0.6 radiation.3
  104.3 0.7 copy-done.2
  105.0 0.7 copy-done.3
  105.7 0.6 reshape.29.icol_ref
  106.3 0.6 reshape.30.iweight_ref
  106.9 0.5 copy-done.13
  107.5 0.1 copy-done.8
  107.5 1.8 merge.1
  109.3 103.9 %all-gather = f32[4,4,128]{2,1,0:T(4,128)} all-gather(f32[1,4,128]{2,1,0:T(4,128)} %bitcast.35), channel_id=1, replica_groups=mesh['atm'=8,'cpl'=4] {'cpl'}, dimensions={0}, use_global_device_ids=true | all-gather | bytes 10240 | tf_op jit(solution)/shard_map/all_gather | solution.py:271
  213.2 1.5 ocean.1
  214.7 5.8 %all-gather.1 = f32[4,4,128]{2,1,0:T(4,128)} all-gather(f32[1,4,128]{2,1,0:T(4,128)} %bitcast.30), channel_id=1, replica_groups=mesh['atm'=8,'cpl'=4] {'cpl'}, dimensions={0}, use_global_device_ids=true | all-gather | bytes 10240 | tf_op jit(solution)/shard_map/all_gather | solution.py:277
  220.5 1.4 column.1
  (27 shorter events, 0.1 us)
Async XLA Ops:
  1.3 2.2 copy-start
  3.5 0.7 copy-start.5
  4.2 5.5 %copy-start.9 = (bf16[32,256]{1,0:T(8,128)(2,1)S(1)}, bf16[32,256]{1,0:T(8,128)(2,1)}, u32[]{:S(2)}) copy-start(bf16[32,256]{1,0:T(8,128)(2,1)} %param.13) | copy-start | bytes 49156
  4.2 5.6 %copy-start.10 = (bf16[32,256]{1,0:T(8,128)(2,1)S(1)}, bf16[32,256]{1,0:T(8,128)(2,1)}, u32[]{:S(2)}) copy-start(bf16[32,256]{1,0:T(8,128)(2,1)} %param.14) | copy-start | bytes 49156
  7.2 94.2 %copy-start.4 = (s32[520]{0:T(1024)}, s32[520]{0:T(1024)S(1)}, u32[]{:S(2)}) copy-start(s32[520]{0:T(1024)S(1)} %get-tuple-element.13.order_ref) | copy-start | bytes 6244
  7.2 94.2 %copy-start.7 = (s32[8]{0:T(128)}, s32[8]{0:T(128)S(1)}, u32[]{:S(2)}) copy-start(s32[8]{0:T(128)S(1)} %get-tuple-element.14.count_ref.meta_ref) | copy-start | bytes 100
  7.3 53.2 %copy-start.6 = (f32[256]{0:T(256)S(1)}, f32[256]{0:T(256)}, u32[]{:S(2)}) copy-start(f32[256]{0:T(256)} %param.15) | copy-start | bytes 3076
  7.3 53.2 %collective-permute-start.1 = (bf16[144,32,128]{2,1,0:T(8,128)(2,1)S(1)}, bf16[144,32,128]{2,1,0:T(8,128)(2,1)S(1)}, u32[]{:S(2)}, u32[]{:S(2)}) collective-permute-start(bf16[144,32,128]{2,1,0:T(8,128)(2,1)S(1)} %get-tuple-element.16), channel_id=1, source_target_pairs={{0,16},{4,20},{8,24},{12,28},{16,0},{20,4},{24,8},{28,12},{1,17},{... | collective-permute-start | bytes 3538952 | tf_op jit(solution)/shard_map/ppermute | solution.py:221
  9.2 50.7 %collective-permute-start = (f32[144]{0:T(256)S(1)}, f32[144]{0:T(256)S(1)}, u32[]{:S(2)}, u32[]{:S(2)}) collective-permute-start(f32[144]{0:T(256)S(1)} %get-tuple-element.15), channel_id=1, source_target_pairs={{0,16},{4,20},{8,24},{12,28},{16,0},{20,4},{24,8},{28,12},{1,17},{... | collective-permute-start | bytes 1736 | tf_op jit(solution)/shard_map/ppermute | solution.py:222
  99.0 7.9 %collective-permute-start.2 = (f32[144]{0:T(256)S(1)}, f32[144]{0:T(256)S(1)}, u32[]{:S(2)}, u32[]{:S(2)}) collective-permute-start(f32[144]{0:T(256)S(1)} %reduce_sum.19), channel_id=1, source_target_pairs={{0,16},{4,20},{8,24},{12,28},{16,0},{20,4},{24,8},{28,12},{1,17},{... | collective-permute-start | bytes 1736 | tf_op jit(solution)/shard_map/ppermute | solution.py:230
  99.1 7.8 %collective-permute-start.3 = (f32[144,128]{1,0:T(8,128)S(1)}, f32[144,128]{1,0:T(8,128)S(1)}, u32[]{:S(2)}, u32[]{:S(2)}) collective-permute-start(f32[144,128]{1,0:T(8,128)S(1)} %get-tuple-element.20), channel_id=1, source_target_pairs={{0,16},{4,20},{8,24},{12,28},{16,0},{20,4},{24,8},{28,12},{1,17},{... | collective-permute-start | bytes 221192 | tf_op jit(solution)/shard_map/ppermute | solution.py:229
  101.4 2.2 copy-start.1
  103.6 2.1 copy-start.11
  103.6 2.7 %copy-start.12 = (s32[512,4]{0,1:T(4,128)S(1)}, s32[512,4]{0,1:T(4,128)}, u32[]{:S(2)}) copy-start(s32[512,4]{0,1:T(4,128)} %param.18) | copy-start | bytes 24580
  104.3 0.7 copy-start.2
  105.0 0.7 copy-start.3
  106.9 0.6 copy-start.13
  106.9 0.6 copy-start.8

commit v3 on v2

--- a/solution.py
+++ b/solution.py
@@ -221,6 +221,7 @@
     guest = lax.ppermute(packed, "atm", swap)
     guest_cosine = lax.ppermute(sent, "atm", swap)
     heat, part = radiation(order, meta, cosine, state, constants)
+    guest, guest_cosine, heat, part = lax.optimization_barrier((guest, guest_cosine, heat, part))
     guest_count = jnp.sum((guest_cosine > 0).astype(jnp.int32)).reshape(1)
     guest_heat, guest_part = radiation(
         jnp.arange(moved_cols, dtype=jnp.int32), guest_count, guest_cosine, guest, constants

time: 222 us -> 138 us (0.62)
  blocking collectives: 110 us -> 15.6 us
  Pallas kernels: 46.6 us -> 105 us
  waiting for transfers between devices: 49.5 us -> 0.51 us
    all_gather x1, blocking collectives: 104 us -> 9.79 us  [local(): section_flux = lax.all_gather(surface, 'cpl', axis=0, tiled=True)]
    pallas_call x2, Pallas kernels: 38.9 us -> 97.2 us  [radiation(): pl.pallas_call(radiation_kernel, out_shape=(jax.ShapeDtypeStruct((columns...]
    ppermute x1, waiting for transfers between devices: 49.5 us -> 0.01 us  [balanced(): guest_cosine = lax.ppermute(sent, 'atm', swap)]
    ppermute x1, starting transfers between devices: 0.07 us -> 2.41 us  [balanced(): surf_back = lax.ppermute(guest_surf, 'atm', swap)]
    ppermute x1, starting transfers between devices: 2.35 us -> 0.07 us  [balanced(): back = lax.ppermute(guest_heat, 'atm', swap)]
  transfers between devices with their start and end apart: 4 -> 4, of which waited for: 1 -> 1; matrix products, arithmetic and copies ran while one was open for 1% -> 1% of each run, Pallas kernels for 0% -> 70%
where the time goes in v3:
time: 138 us; the launch traced here: 137 us
  Pallas kernels  105 us (76%)
  blocking collectives  15.6 us (11%)
  local copies, waits for them, and re-layouts  7.78 us (6%)
  starting transfers between devices  5.39 us (4%)
  other arithmetic  1.84 us (1%)
    pallas_call x2, Pallas kernels, radiation(): pl.pallas_call(radiation_kernel, out_shape=(jax.ShapeDtypeStruct((columns...  97.2 us
    all_gather x1, blocking collectives, local(): section_flux = lax.all_gather(surface, 'cpl', axis=0, tiled=True)  9.79 us
    unnamed x28, local copies, waits for them, and re-layouts  6.27 us
    all_gather x1, blocking collectives, local(): section_sea = lax.all_gather(sea_next, 'cpl', axis=0, tiled=True)  5.81 us
    ppermute x1, starting transfers between devices, balanced(): guest = lax.ppermute(packed, 'atm', swap)  2.83 us
  transfers between devices with their start and end apart: 4, of which 1 were waited for; matrix products, arithmetic and copies ran while one was open for 1% of the time, Pallas kernels for 70%

profile of v3, /device:TPU:9, one launch (start us, length us, event | category | flops | bytes accessed | tf_op | source)
XLA Modules:
  0.0 136.6 jit_solution(8137754021098604956)
XLA Ops:
  0.6 0.7 convert_element_type.21.cosine_ref
  1.3 2.2 %copy-done = bf16[512,32,128]{2,1,0:T(8,128)(2,1)S(1)} copy-done((bf16[512,32,128]{2,1,0:T(8,128)(2,1)S(1)}, bf16[512,32,128]{2,1,0:T(8,128)(2,1)}, u32[]{:S(2)}) %copy-start) | copy-done | bytes 4194328
  3.5 0.7 copy-done.5
  4.2 2.6 %pack.1 = (bf16[144,32,128]{2,1,0:T(8,128)(2,1)S(1)}, f32[144]{0:T(256)S(1)}, s32[520]{0:T(1024)S(1)}, s32[8]{0:T(128)S(1)}) custom-call(s32[512]{0:T(512)S(1)} %copy-done.5, f32[512]{0:T(512)S(1)} %convert_element_type.21.cosine_ref, bf16[512,32,128]{2,1,0:T(8,128)(2,1)S(1)} %copy-done), custom_call_target="tpu_custom_call" | custom-call | tf_op jit(solution)/shard_map/pack/pallas_call | solution.py:161
  6.8 0.0 copy-start.6
  6.8 2.8 %collective-permute-start = (bf16[144,32,128]{2,1,0:T(8,128)(2,1)S(1)}, bf16[144,32,128]{2,1,0:T(8,128)(2,1)S(1)}, u32[]{:S(2)}, u32[]{:S(2)}) collective-permute-start(bf16[144,32,128]{2,1,0:T(8,128)(2,1)S(1)} %get-tuple-element.19), channel_id=1, source_target_pairs={{0,16},{4,20},{8,24},{12,28},{16,0},{20,4},{24,8},{28,12},{1,17},{... | collective-permute-start | bytes 3538952 | tf_op jit(solution)/shard_map/ppermute | solution.py:221
  9.6 0.1 collective-permute-start.1
  9.7 0.1 copy.17
  9.9 0.1 copy.18
  10.1 0.2 fusion.1.upper_ref
  10.2 0.1 pad_maximum_fusion
  10.4 0.1 broadcast_in_dim.4.wide_ref
  10.5 0.0 copy-start.1
  10.5 2.2 %copy-done.1 = bf16[512,32,128]{2,1,0:T(8,128)(2,1)S(1)} copy-done((bf16[512,32,128]{2,1,0:T(8,128)(2,1)S(1)}, bf16[512,32,128]{2,1,0:T(8,128)(2,1)}, u32[]{:S(2)}) %copy-start.1) | copy-done | bytes 4194328
  12.7 95.9 %radiation.2 = (f32[512,128]{1,0:T(8,128)S(1)}, f32[512,128]{1,0:T(8,128)S(1)}) custom-call(s32[520]{0:T(1024)S(1)} %get-tuple-element.17.order_ref, s32[8]{0:T(128)S(1)} %get-tuple-element.18.count_ref.meta_ref, f32[512]{0:T(512)S(1)} %convert_element_type.21.cosine_ref, bf16[512,32,128]{2,1,0:T(8,128)(2,1)S(1)} %copy-done.1, ...), custom_call_target="tpu_custom_call" | custom-call | flops 16777216000 | bytes 4194304 | tf_op jit(solution)/shard_map/radiation/pallas_call | solution.py:179
  108.7 0.0 collective-permute-done.1.cosine_ref
  108.7 0.0 collective-permute-done.state_ref
  108.7 0.6 fusion.4
  109.3 1.2 radiation.3
  110.6 0.1 collective-permute-start.3
  110.7 0.1 reduce_sum.19
  110.8 2.4 %collective-permute-start.2 = (f32[144]{0:T(256)S(1)}, f32[144]{0:T(256)S(1)}, u32[]{:S(2)}, u32[]{:S(2)}) collective-permute-start(f32[144]{0:T(256)S(1)} %reduce_sum.19), channel_id=1, source_target_pairs={{0,16},{4,20},{8,24},{12,28},{16,0},{20,4},{24,8},{28,12},{1,17},{... | collective-permute-start | bytes 1736 | tf_op jit(solution)/shard_map/ppermute | solution.py:231
  113.2 0.6 reshape.29.icol_ref
  113.8 0.6 reshape.30.iweight_ref
  114.4 0.5 collective-permute-done.2.surf_in_ref
  114.9 0.6 copy-done.13
  115.5 0.6 copy-done.8
  116.1 2.1 %merge.1 = (f32[512,128]{1,0:T(8,128)}, f32[4,128]{1,0:T(4,128)}) custom-call(s32[520]{0:T(1024)} %copy-done.4, s32[8]{0:T(128)} %copy-done.7, f32[144]{0:T(256)} %copy-done.13, f32[512,128]{1,0:T(8,128)} %copy-done.2, f32[512,128]{1,0:T(8,128)} %copy-done.3, f32[144,128]{1,0:T(8,128)} %copy-done.8), custom_call_target="tpu_custom_call" | custom-call | tf_op jit(solution)/shard_map/merge/pallas_call | solution.py:202
  118.2 9.8 %all-gather = f32[4,4,128]{2,1,0:T(4,128)} all-gather(f32[1,4,128]{2,1,0:T(4,128)} %bitcast.35), channel_id=1, replica_groups=mesh['atm'=8,'cpl'=4] {'cpl'}, dimensions={0}, use_global_device_ids=true | all-gather | bytes 10240 | tf_op jit(solution)/shard_map/all_gather | solution.py:272
  128.0 1.5 %ocean.1 = f32[4,128]{1,0:T(4,128)} custom-call(f32[16,128]{1,0:T(8,128)} %bitcast.28, s32[16,128]{1,0:T(8,128)} %reshape.29.icol_ref, s32[16,128]{1,0:T(8,128)} %reshape.30.iweight_ref, f32[4,128]{1,0:T(4,128)} %bitcast.34), custom_call_target="tpu_custom_call" | custom-call | tf_op jit(solution)/shard_map/ocean/pallas_call | solution.py:273
  129.5 5.8 %all-gather.1 = f32[4,4,128]{2,1,0:T(4,128)} all-gather(f32[1,4,128]{2,1,0:T(4,128)} %bitcast.30), channel_id=1, replica_groups=mesh['atm'=8,'cpl'=4] {'cpl'}, dimensions={0}, use_global_device_ids=true | all-gather | bytes 10240 | tf_op jit(solution)/shard_map/all_gather | solution.py:278
  135.3 1.4 %column.1 = f32[4,128]{1,0:T(4,128)} custom-call(f32[16,128]{1,0:T(8,128)} %bitcast.29, s32[4,128]{1,0:T(4,128)} %bitcast.36), custom_call_target="tpu_custom_call" | custom-call | tf_op jit(solution)/shard_map/column/pallas_call | solution.py:279
  (27 shorter events, 0.1 us)
Async XLA Ops:
  1.3 2.2 %copy-start = (bf16[512,32,128]{2,1,0:T(8,128)(2,1)S(1)}, bf16[512,32,128]{2,1,0:T(8,128)(2,1)}, u32[]{:S(2)}) copy-start(bf16[512,32,128]{2,1,0:T(8,128)(2,1)} %state_ref.3) | copy-start | bytes 12582916
  3.5 0.7 copy-start.5
  4.2 5.5 %copy-start.9 = (bf16[32,256]{1,0:T(8,128)(2,1)S(1)}, bf16[32,256]{1,0:T(8,128)(2,1)}, u32[]{:S(2)}) copy-start(bf16[32,256]{1,0:T(8,128)(2,1)} %param.13) | copy-start | bytes 49156
  4.2 5.7 %copy-start.10 = (bf16[32,256]{1,0:T(8,128)(2,1)S(1)}, bf16[32,256]{1,0:T(8,128)(2,1)}, u32[]{:S(2)}) copy-start(bf16[32,256]{1,0:T(8,128)(2,1)} %param.14) | copy-start | bytes 49156
  6.8 101.8 %copy-start.4 = (s32[520]{0:T(1024)}, s32[520]{0:T(1024)S(1)}, u32[]{:S(2)}) copy-start(s32[520]{0:T(1024)S(1)} %get-tuple-element.17.order_ref) | copy-start | bytes 6244
  6.8 101.8 %copy-start.7 = (s32[8]{0:T(128)}, s32[8]{0:T(128)S(1)}, u32[]{:S(2)}) copy-start(s32[8]{0:T(128)S(1)} %get-tuple-element.18.count_ref.meta_ref) | copy-start | bytes 100
  6.8 3.6 %copy-start.6 = (f32[256]{0:T(256)S(1)}, f32[256]{0:T(256)}, u32[]{:S(2)}) copy-start(f32[256]{0:T(256)} %param.15) | copy-start | bytes 3076
  6.8 101.9 %collective-permute-start = (bf16[144,32,128]{2,1,0:T(8,128)(2,1)S(1)}, bf16[144,32,128]{2,1,0:T(8,128)(2,1)S(1)}, u32[]{:S(2)}, u32[]{:S(2)}) collective-permute-start(bf16[144,32,128]{2,1,0:T(8,128)(2,1)S(1)} %get-tuple-element.19), channel_id=1, source_target_pairs={{0,16},{4,20},{8,24},{12,28},{16,0},{20,4},{24,8},{28,12},{1,17},{... | collective-permute-start | bytes 3538952 | tf_op jit(solution)/shard_map/ppermute | solution.py:221
  9.6 99.0 %collective-permute-start.1 = (f32[144]{0:T(256)S(1)}, f32[144]{0:T(256)S(1)}, u32[]{:S(2)}, u32[]{:S(2)}) collective-permute-start(f32[144]{0:T(256)S(1)} %get-tuple-element.20), channel_id=1, source_target_pairs={{0,16},{4,20},{8,24},{12,28},{16,0},{20,4},{24,8},{28,12},{1,17},{... | collective-permute-start | bytes 1736 | tf_op jit(solution)/shard_map/ppermute | solution.py:222
  10.5 2.2 %copy-start.1 = (bf16[512,32,128]{2,1,0:T(8,128)(2,1)S(1)}, bf16[512,32,128]{2,1,0:T(8,128)(2,1)}, u32[]{:S(2)}) copy-start(bf16[512,32,128]{2,1,0:T(8,128)(2,1)} %state_ref.3) | copy-start | bytes 12582916
  108.6 1.9 %copy-start.2 = (f32[512,128]{1,0:T(8,128)}, f32[512,128]{1,0:T(8,128)S(1)}, u32[]{:S(2)}) copy-start(f32[512,128]{1,0:T(8,128)S(1)} %get-tuple-element.26.heat_in_ref) | copy-start | bytes 786436
  108.7 1.9 %copy-start.3 = (f32[512,128]{1,0:T(8,128)}, f32[512,128]{1,0:T(8,128)S(1)}, u32[]{:S(2)}) copy-start(f32[512,128]{1,0:T(8,128)S(1)} %get-tuple-element.27.part_in_ref) | copy-start | bytes 786436
  109.3 3.9 %copy-start.11 = (s32[512,4]{0,1:T(4,128)S(1)}, s32[512,4]{0,1:T(4,128)}, u32[]{:S(2)}) copy-start(s32[512,4]{0,1:T(4,128)} %param.17) | copy-start | bytes 24580
  109.3 4.5 %copy-start.12 = (s32[512,4]{0,1:T(4,128)S(1)}, s32[512,4]{0,1:T(4,128)}, u32[]{:S(2)}) copy-start(s32[512,4]{0,1:T(4,128)} %param.18) | copy-start | bytes 24580
  110.6 4.3 %collective-permute-start.3 = (f32[144,128]{1,0:T(8,128)S(1)}, f32[144,128]{1,0:T(8,128)S(1)}, u32[]{:S(2)}, u32[]{:S(2)}) collective-permute-start(f32[144,128]{1,0:T(8,128)S(1)} %get-tuple-element.28), channel_id=1, source_target_pairs={{0,16},{4,20},{8,24},{12,28},{16,0},{20,4},{24,8},{28,12},{1,17},{... | collective-permute-start | bytes 221192 | tf_op jit(solution)/shard_map/ppermute | solution.py:230
  110.8 4.1 %collective-permute-start.2 = (f32[144]{0:T(256)S(1)}, f32[144]{0:T(256)S(1)}, u32[]{:S(2)}, u32[]{:S(2)}) collective-permute-start(f32[144]{0:T(256)S(1)} %reduce_sum.19), channel_id=1, source_target_pairs={{0,16},{4,20},{8,24},{12,28},{16,0},{20,4},{24,8},{28,12},{1,17},{... | collective-permute-start | bytes 1736 | tf_op jit(solution)/shard_map/ppermute | solution.py:231
  114.9 0.6 copy-start.13
  115.5 0.6 copy-start.8

commit v4 on v3

--- a/solution.py
+++ b/solution.py
@@ -11,7 +11,7 @@
 relax_keep = 0.75
 forcing = 4.0
 group_cols = 8
-moved_cols = 144
+moved_cols = 152
 chunk_g = 64
 log2e = 1.4426950408889634
 ln2 = 0.6931471805599453
@@ -76,11 +76,11 @@
 
 
 def radiation_kernel(
-    order_ref, count_ref, cosine_ref, state_ref, kabs_ref, ksca_ref, upper_ref, wide_ref, weight_ref,
+    order_ref, count_ref, cosine_ref, state_ref, kboth_ref, upper_ref, wide_ref, weight_ref,
     heat_ref, part_ref, ext_ref,
 ):
     columns, levels = heat_ref.shape
-    gpoints = kabs_ref.shape[0]
+    gpoints = wide_ref.shape[0]
     heat_ref[...] = jnp.zeros_like(heat_ref)
     part_ref[...] = jnp.zeros_like(part_ref)
     count = count_ref[0]
@@ -103,12 +103,12 @@
             total = jnp.zeros((8, 2 * levels), jnp.float32)
             for low in range(0, gpoints, chunk_g):
                 rows = slice(low, low + chunk_g)
-                soft_abs = soft_plus2(
-                    jnp.dot(kabs_ref[rows], both, preferred_element_type=jnp.float32)
+                proj = jnp.dot(
+                    kboth_ref[2 * low : 2 * low + 2 * chunk_g], both,
+                    preferred_element_type=jnp.float32,
                 )
-                soft_sca = soft_plus2(
-                    jnp.dot(ksca_ref[rows], both, preferred_element_type=jnp.float32)
-                )
+                soft_abs = soft_plus2(proj[:chunk_g])
+                soft_sca = soft_plus2(proj[chunk_g:])
                 soft = soft_abs + soft_sca
                 ext = ((depth_scale * ln2) * soft).astype(jnp.bfloat16)
                 ext_ref[pair, rows] = ext
@@ -149,7 +149,9 @@
     same = (row_index // levels) == (col_index // levels)
     upper = (same & (row_index <= col_index)).astype(jnp.bfloat16)
     wide = jnp.broadcast_to(weights[:, None], (weights.shape[0], 2 * levels))
-    return split_terms(kcoef), split_terms(scatter_coef), upper, wide, weights[None, :]
+    pieces = jnp.stack([split_terms(kcoef), split_terms(scatter_coef)])
+    pieces = pieces.reshape(2, -1, chunk_g, pieces.shape[2]).transpose(1, 0, 2, 3)
+    return pieces.reshape(-1, pieces.shape[3]), upper, wide, weights[None, :]
 
 
 vmem = pl.BlockSpec(memory_space=pltpu.VMEM)
@@ -175,14 +177,14 @@
 
 def radiation(order, count, cosine, state, constants):
     columns, feats, levels = state.shape
-    gpoints = constants[0].shape[0]
+    gpoints = constants[2].shape[0]
     return pl.pallas_call(
         radiation_kernel,
         out_shape=(
             jax.ShapeDtypeStruct((columns, levels), jnp.float32),
             jax.ShapeDtypeStruct((columns, 128), jnp.float32),
         ),
-        in_specs=[smem, smem, smem, vmem, vmem, vmem, vmem, vmem, vmem],
+        in_specs=[smem, smem, smem, vmem, vmem, vmem, vmem, vmem],
         out_specs=(vmem, vmem),
         scratch_shapes=[
             pltpu.VMEM((group_cols // 2, gpoints, 2 * levels), jnp.bfloat16),

time: 138 us -> 132 us (0.957)
  Pallas kernels: 105 us -> 82.4 us
  starting transfers between devices: 5.39 us -> 20.2 us
  blocking collectives: 15.6 us -> 13.5 us
  waiting for transfers between devices: 0.51 us -> 2.39 us
    pallas_call x2, Pallas kernels: 97.2 us -> 74.8 us  [radiation(): pl.pallas_call(radiation_kernel, out_shape=(jax.ShapeDtypeStruct((columns...]
    ppermute x1, starting transfers between devices: 0.07 us -> 17.1 us  [balanced(): back = lax.ppermute(guest_heat, 'atm', swap)]
    all_gather x1, blocking collectives: 9.79 us -> 7.26 us  [local(): section_flux = lax.all_gather(surface, 'cpl', axis=0, tiled=True)]
    ppermute x1, starting transfers between devices: 2.41 us -> 0.08 us  [balanced(): surf_back = lax.ppermute(guest_surf, 'atm', swap)]
    ppermute x1, waiting for transfers between devices: 0.5 us -> 2.39 us  [balanced(): surf_back = lax.ppermute(guest_surf, 'atm', swap)]
  transfers between devices with their start and end apart: 4 -> 4, of which waited for: 1 -> 1; matrix products, arithmetic and copies ran while one was open for 1% -> 2% of each run, Pallas kernels for 70% -> 57%
where the time goes in v4:
time: 132 us; the launch traced here: 129 us
  Pallas kernels  82.4 us (62%)
  starting transfers between devices  20.2 us (15%)
  blocking collectives  13.5 us (10%)
  local copies, waits for them, and re-layouts  8.29 us (6%)
  waiting for transfers between devices  2.39 us (2%)
  other arithmetic  1.79 us (1%)
    pallas_call x2, Pallas kernels, radiation(): pl.pallas_call(radiation_kernel, out_shape=(jax.ShapeDtypeStruct((columns...  74.8 us
    ppermute x1, starting transfers between devices, balanced(): back = lax.ppermute(guest_heat, 'atm', swap)  17.1 us
    all_gather x1, blocking collectives, local(): section_flux = lax.all_gather(surface, 'cpl', axis=0, tiled=True)  7.26 us
    unnamed x28, local copies, waits for them, and re-layouts  6.28 us
    all_gather x1, blocking collectives, local(): section_sea = lax.all_gather(sea_next, 'cpl', axis=0, tiled=True)  6.27 us
    ppermute x1, starting transfers between devices, balanced(): guest = lax.ppermute(packed, 'atm', swap)  2.85 us
  transfers between devices with their start and end apart: 4, of which 1 were waited for; matrix products, arithmetic and copies ran while one was open for 2% of the time, Pallas kernels for 57%

profile of v4, /device:TPU:9, one launch (start us, length us, event | category | flops | bytes accessed | tf_op | source)
XLA Modules:
  0.0 129.4 jit_solution(6397029452801769855)
XLA Ops:
  0.6 0.7 convert_element_type.37.cosine_ref
  1.3 2.2 %copy-done = bf16[512,32,128]{2,1,0:T(8,128)(2,1)S(1)} copy-done((bf16[512,32,128]{2,1,0:T(8,128)(2,1)S(1)}, bf16[512,32,128]{2,1,0:T(8,128)(2,1)}, u32[]{:S(2)}) %copy-start) | copy-done | bytes 4194328
  3.5 0.7 copy-done.5
  4.2 2.6 %pack.1 = (bf16[152,32,128]{2,1,0:T(8,128)(2,1)S(1)}, f32[152]{0:T(256)S(1)}, s32[520]{0:T(1024)S(1)}, s32[8]{0:T(128)S(1)}) custom-call(s32[512]{0:T(512)S(1)} %copy-done.5, f32[512]{0:T(512)S(1)} %convert_element_type.37.cosine_ref, bf16[512,32,128]{2,1,0:T(8,128)(2,1)S(1)} %copy-done), custom_call_target="tpu_custom_call" | custom-call | tf_op jit(solution)/shard_map/pack/pallas_call | solution.py:163
  6.8 2.9 %collective-permute-start = (bf16[152,32,128]{2,1,0:T(8,128)(2,1)S(1)}, bf16[152,32,128]{2,1,0:T(8,128)(2,1)S(1)}, u32[]{:S(2)}, u32[]{:S(2)}) collective-permute-start(bf16[152,32,128]{2,1,0:T(8,128)(2,1)S(1)} %get-tuple-element.19), channel_id=1, source_target_pairs={{0,16},{4,20},{8,24},{12,28},{16,0},{20,4},{24,8},{28,12},{1,17},{... | collective-permute-start | bytes 3735560 | tf_op jit(solution)/shard_map/ppermute | solution.py:223
  9.7 0.1 collective-permute-start.1
  9.8 0.1 copy.30
  9.9 0.1 copy.29
  10.0 0.1 copy.28
  10.2 0.1 copy.27
  10.3 0.1 copy.26
  10.4 0.1 copy.25
  10.6 0.2 fusion.1.upper_ref
  10.7 0.1 maximum_maximum_fusion
  10.9 0.1 broadcast_in_dim.4.wide_ref
  11.0 2.2 %copy-done.1 = bf16[512,32,128]{2,1,0:T(8,128)(2,1)S(1)} copy-done((bf16[512,32,128]{2,1,0:T(8,128)(2,1)S(1)}, bf16[512,32,128]{2,1,0:T(8,128)(2,1)}, u32[]{:S(2)}) %copy-start.1) | copy-done | bytes 4194328
  13.2 73.6 %radiation.2 = (f32[512,128]{1,0:T(8,128)S(1)}, f32[512,128]{1,0:T(8,128)S(1)}) custom-call(s32[520]{0:T(1024)S(1)} %get-tuple-element.17.order_ref, s32[8]{0:T(128)S(1)} %get-tuple-element.18.count_ref.meta_ref, f32[512]{0:T(512)S(1)} %convert_element_type.37.cosine_ref, bf16[512,32,128]{2,1,0:T(8,128)(2,1)S(1)} %copy-done.1, bf16[512,96]{1,0:T(8,128)(2,1)S(1)} %bitcast.35, ...), custom_call_target="tpu_custom_call" | custom-call | flops 16777216000 | bytes 4194304 | tf_op jit(solution)/shard_map/radiation/pallas_call | solution.py:181
  86.8 0.6 fusion.4
  87.5 1.2 radiation.3
  88.7 17.1 %collective-permute-start.3 = (f32[152,128]{1,0:T(8,128)S(1)}, f32[152,128]{1,0:T(8,128)S(1)}, u32[]{:S(2)}, u32[]{:S(2)}) collective-permute-start(f32[152,128]{1,0:T(8,128)S(1)} %get-tuple-element.28), channel_id=1, source_target_pairs={{0,16},{4,20},{8,24},{12,28},{16,0},{20,4},{24,8},{28,12},{1,17},{... | collective-permute-start | bytes 233480 | tf_op jit(solution)/shard_map/ppermute | solution.py:232
  105.9 0.1 reduce_sum.19
  106.0 0.1 collective-permute-start.2
  106.1 0.6 reshape.138.icol_ref
  106.7 0.6 reshape.139.iweight_ref
  107.3 2.4 %collective-permute-done.2.surf_in_ref = f32[152]{0:T(256)S(1)} collective-permute-done((f32[152]{0:T(256)S(1)}, f32[152]{0:T(256)S(1)}, u32[]{:S(2)}, u32[]{:S(2)}) %collective-permute-start.2) | collective-permute-done | bytes 640 | tf_op jit(solution)/shard_map/ppermute | solution.py:233
  109.7 0.6 copy-done.13
  110.3 0.6 copy-done.8
  110.9 2.1 %merge.1 = (f32[512,128]{1,0:T(8,128)}, f32[4,128]{1,0:T(4,128)}) custom-call(s32[520]{0:T(1024)} %copy-done.4, s32[8]{0:T(128)} %copy-done.7, f32[152]{0:T(256)} %copy-done.13, f32[512,128]{1,0:T(8,128)} %copy-done.2, f32[512,128]{1,0:T(8,128)} %copy-done.3, f32[152,128]{1,0:T(8,128)} %copy-done.8), custom_call_target="tpu_custom_call" | custom-call | tf_op jit(solution)/shard_map/merge/pallas_call | solution.py:204
  113.0 7.3 %all-gather = f32[4,4,128]{2,1,0:T(4,128)} all-gather(f32[1,4,128]{2,1,0:T(4,128)} %bitcast.52), channel_id=1, replica_groups=mesh['atm'=8,'cpl'=4] {'cpl'}, dimensions={0}, use_global_device_ids=true | all-gather | bytes 10240 | tf_op jit(solution)/shard_map/all_gather | solution.py:274
  120.3 1.5 %ocean.1 = f32[4,128]{1,0:T(4,128)} custom-call(f32[16,128]{1,0:T(8,128)} %bitcast.45, s32[16,128]{1,0:T(8,128)} %reshape.138.icol_ref, s32[16,128]{1,0:T(8,128)} %reshape.139.iweight_ref, f32[4,128]{1,0:T(4,128)} %bitcast.51), custom_call_target="tpu_custom_call" | custom-call | tf_op jit(solution)/shard_map/ocean/pallas_call | solution.py:275
  121.7 6.3 %all-gather.1 = f32[4,4,128]{2,1,0:T(4,128)} all-gather(f32[1,4,128]{2,1,0:T(4,128)} %bitcast.47), channel_id=1, replica_groups=mesh['atm'=8,'cpl'=4] {'cpl'}, dimensions={0}, use_global_device_ids=true | all-gather | bytes 10240 | tf_op jit(solution)/shard_map/all_gather | solution.py:280
  128.0 1.4 %column.1 = f32[4,128]{1,0:T(4,128)} custom-call(f32[16,128]{1,0:T(8,128)} %bitcast.46, s32[4,128]{1,0:T(4,128)} %bitcast.53), custom_call_target="tpu_custom_call" | custom-call | tf_op jit(solution)/shard_map/column/pallas_call | solution.py:281
  (31 shorter events, 0.1 us)
Async XLA Ops:
  1.3 2.2 %copy-start = (bf16[512,32,128]{2,1,0:T(8,128)(2,1)S(1)}, bf16[512,32,128]{2,1,0:T(8,128)(2,1)}, u32[]{:S(2)}) copy-start(bf16[512,32,128]{2,1,0:T(8,128)(2,1)} %state_ref.3) | copy-start | bytes 12582916
  3.5 0.7 copy-start.5
  4.2 5.6 %copy-start.9 = (bf16[32,256]{1,0:T(8,128)(2,1)S(1)}, bf16[32,256]{1,0:T(8,128)(2,1)}, u32[]{:S(2)}) copy-start(bf16[32,256]{1,0:T(8,128)(2,1)} %param.14) | copy-start | bytes 49156
  4.2 6.0 %copy-start.10 = (bf16[32,256]{1,0:T(8,128)(2,1)S(1)}, bf16[32,256]{1,0:T(8,128)(2,1)}, u32[]{:S(2)}) copy-start(bf16[32,256]{1,0:T(8,128)(2,1)} %param.13) | copy-start | bytes 49156
  6.8 80.0 %copy-start.4 = (s32[520]{0:T(1024)}, s32[520]{0:T(1024)S(1)}, u32[]{:S(2)}) copy-start(s32[520]{0:T(1024)S(1)} %get-tuple-element.17.order_ref) | copy-start | bytes 6244
  6.8 80.0 %copy-start.7 = (s32[8]{0:T(128)}, s32[8]{0:T(128)S(1)}, u32[]{:S(2)}) copy-start(s32[8]{0:T(128)S(1)} %get-tuple-element.18.count_ref.meta_ref) | copy-start | bytes 100
  6.8 4.1 %copy-start.6 = (f32[256]{0:T(256)S(1)}, f32[256]{0:T(256)}, u32[]{:S(2)}) copy-start(f32[256]{0:T(256)} %param.15) | copy-start | bytes 3076
  6.8 80.0 %collective-permute-start = (bf16[152,32,128]{2,1,0:T(8,128)(2,1)S(1)}, bf16[152,32,128]{2,1,0:T(8,128)(2,1)S(1)}, u32[]{:S(2)}, u32[]{:S(2)}) collective-permute-start(bf16[152,32,128]{2,1,0:T(8,128)(2,1)S(1)} %get-tuple-element.19), channel_id=1, source_target_pairs={{0,16},{4,20},{8,24},{12,28},{16,0},{20,4},{24,8},{28,12},{1,17},{... | collective-permute-start | bytes 3735560 | tf_op jit(solution)/shard_map/ppermute | solution.py:223
  9.7 77.1 %collective-permute-start.1 = (f32[152]{0:T(256)S(1)}, f32[152]{0:T(256)S(1)}, u32[]{:S(2)}, u32[]{:S(2)}) collective-permute-start(f32[152]{0:T(256)S(1)} %get-tuple-element.20), channel_id=1, source_target_pairs={{0,16},{4,20},{8,24},{12,28},{16,0},{20,4},{24,8},{28,12},{1,17},{... | collective-permute-start | bytes 1832 | tf_op jit(solution)/shard_map/ppermute | solution.py:224
  11.0 2.2 %copy-start.1 = (bf16[512,32,128]{2,1,0:T(8,128)(2,1)S(1)}, bf16[512,32,128]{2,1,0:T(8,128)(2,1)}, u32[]{:S(2)}) copy-start(bf16[512,32,128]{2,1,0:T(8,128)(2,1)} %state_ref.3) | copy-start | bytes 12582916
  86.8 1.9 %copy-start.2 = (f32[512,128]{1,0:T(8,128)}, f32[512,128]{1,0:T(8,128)S(1)}, u32[]{:S(2)}) copy-start(f32[512,128]{1,0:T(8,128)S(1)} %get-tuple-element.26.heat_in_ref) | copy-start | bytes 786436
  86.8 1.9 %copy-start.3 = (f32[512,128]{1,0:T(8,128)}, f32[512,128]{1,0:T(8,128)S(1)}, u32[]{:S(2)}) copy-start(f32[512,128]{1,0:T(8,128)S(1)} %get-tuple-element.27.part_in_ref) | copy-start | bytes 786436
  87.5 18.6 %copy-start.11 = (s32[512,4]{0,1:T(4,128)S(1)}, s32[512,4]{0,1:T(4,128)}, u32[]{:S(2)}) copy-start(s32[512,4]{0,1:T(4,128)} %param.17) | copy-start | bytes 24580
  87.5 19.2 %copy-start.12 = (s32[512,4]{0,1:T(4,128)S(1)}, s32[512,4]{0,1:T(4,128)}, u32[]{:S(2)}) copy-start(s32[512,4]{0,1:T(4,128)} %param.18) | copy-start | bytes 24580
  88.7 21.0 %collective-permute-start.3 = (f32[152,128]{1,0:T(8,128)S(1)}, f32[152,128]{1,0:T(8,128)S(1)}, u32[]{:S(2)}, u32[]{:S(2)}) collective-permute-start(f32[152,128]{1,0:T(8,128)S(1)} %get-tuple-element.28), channel_id=1, source_target_pairs={{0,16},{4,20},{8,24},{12,28},{16,0},{20,4},{24,8},{28,12},{1,17},{... | collective-permute-start | bytes 233480 | tf_op jit(solution)/shard_map/ppermute | solution.py:232
  106.0 3.7 %collective-permute-start.2 = (f32[152]{0:T(256)S(1)}, f32[152]{0:T(256)S(1)}, u32[]{:S(2)}, u32[]{:S(2)}) collective-permute-start(f32[152]{0:T(256)S(1)} %reduce_sum.19), channel_id=1, source_target_pairs={{0,16},{4,20},{8,24},{12,28},{16,0},{20,4},{24,8},{28,12},{1,17},{... | collective-permute-start | bytes 1832 | tf_op jit(solution)/shard_map/ppermute | solution.py:233
  109.7 0.6 copy-start.13
  110.3 0.6 copy-start.8
